TPU v7x, 32 devices: a whole 2x2x4 slice. The times are simulated.
32 devices in a mesh: grp: 4 (over x, core), own: 8 (over z, y).
Axes of the slice: x: 2, y: 2, z: 4, core: 2. Of those that a mesh axis runs over, the one named last changes fastest.
Arguments:
- orbitals: bfloat16 [32, 32, 1024], P(('grp', 'own')), may hold values from -3 to 3
- offsets: int32 [32, 2], P(('grp', 'own')), may hold values from 0 to 32
- pairs: int32 [32, 2], P('grp'), may hold values from 0 to 7, as said below
- ext_pot: bfloat16 [32, 4096], replicated, may hold values from -6 to 6
Outputs:
- gradient: float32 [32, 32, 1024], P(('grp', 'own'))
Inputs may be any that keep to these rules, and one draw needn't show every extreme that they name: `pairs`: rows g * 8 to g * 8 + 7 belong to group g; each row names two different orbitals of the group. Calling owner o the device holding orbital o of a group, at most 2 rows of a group have orbital o as their first orbital, and in every group some owner has exactly 2.
All inputs are finite; a program needn't handle non-finite values.
Results may differ from a plain program's by a relative error of at most 0.0006.
Values may be sent and summed in bfloat16 or wider, within the bound.
A program may use at most 64 MiB of HBM per device.

v0:
```python
import functools
import math

import jax
import jax.numpy as jnp
from jax import lax
from jax.experimental import pallas as pl
from jax.experimental.pallas import tpu as pltpu
from jax.sharding import PartitionSpec as P

SCREEN = 0.0025
MIXING = 0.25
EXCHANGE_COEF = (3.0 / math.pi) ** (1.0 / 3.0)
PRECISE = lax.Precision.HIGHEST
SPLIT = lax.Precision.HIGH
VMEM = pltpu.VMEM


def side_of(cells):
    return math.isqrt(cells)


def cas_table(length, count):
    row = lax.broadcasted_iota(jnp.int32, (length, count), 0)
    col = lax.broadcasted_iota(jnp.int32, (length, count), 1)
    angle = 2.0 * math.pi / length * (row * col % length).astype(jnp.float32)
    return jnp.cos(angle) + jnp.sin(angle)


def wave_squares(length):
    positions = jnp.arange(length, dtype=jnp.int32)
    signed = jnp.where(positions < length // 2, positions, positions - length)
    wavenumber = 2.0 * math.pi / length * signed.astype(jnp.float32)
    return wavenumber * wavenumber


def green_table(depth, width):
    along_z = wave_squares(2 * depth)
    along_y = wave_squares(2 * width)
    squared_sum = along_z[:, None, None] + along_y[None, :, None] + along_y[None, None, :]
    return 4.0 * math.pi / (squared_sum + SCREEN)


def rotate(pattern, matrix, operand):
    return jnp.einsum(pattern, matrix, operand, precision=SPLIT, preferred_element_type=jnp.float32)


def placer(starts, row_count, side):
    grid_index = lax.broadcasted_iota(jnp.int32, (starts.shape[0], row_count, side), 1)
    cell_index = lax.broadcasted_iota(jnp.int32, (starts.shape[0], row_count, side), 2)
    return (grid_index == cell_index + starts[:, None, None]).astype(jnp.float32)


def plane_split(count):
    rows = 1 << ((count.bit_length() - 1) // 2)
    return count // rows, rows


def chunk_rows(array):
    rows = array.shape[0]
    if rows <= 8:
        return rows
    return rows // 2 if array.dtype == jnp.bfloat16 else rows // 4


def relay_kernel(count, pieces, exchanged, *refs):
    far, near = plane_split(count)
    sources, slabs = refs[:pieces], refs[pieces : pieces + exchanged]
    refs = refs[pieces + exchanged :]
    targets, landings = refs[:pieces], refs[pieces : pieces + exchanged]
    send_sem, recv_sem, local_sem, slab_send, slab_recv = refs[pieces + exchanged :]
    me = lax.axis_index("own")
    z = me // near
    y = lax.rem(me, near)
    barrier = pltpu.get_barrier_semaphore()

    def across(step):
        return z * near + lax.rem(y + step, near)

    def signal(peer):
        pl.semaphore_signal(barrier, inc=1, device_id={"own": peer}, device_id_type=pl.DeviceIdType.MESH)

    if exchanged:
        for step in range(1, count):
            signal(lax.rem(me + step, count))
        pl.semaphore_wait(barrier, count - 1)
    else:
        for step in range(1, near):
            signal(across(step))
        pl.when(z > 0)(lambda: signal(me - near))
        pl.when(z < far - 1)(lambda: signal(me + near))
        pl.semaphore_wait(barrier, near - 1 + (z > 0).astype(jnp.int32) + (z < far - 1).astype(jnp.int32))

    parts = []
    for piece, source in enumerate(sources):
        rows = source.shape[0]
        size = chunk_rows(source)
        for start_row in range(0, rows, size):
            parts.append((piece, start_row, size, piece > 0 or start_row > 0))
    fronts = [i for i, part in enumerate(parts) if not part[3]]
    backs = [i for i, part in enumerate(parts) if part[3]]

    def copy(index, origin, lane, peer, own):
        piece, start, size, _ = parts[index]
        rows = pl.ds(start, size)
        source = sources[piece].at[rows] if own else targets[piece].at[origin, rows]
        return pltpu.make_async_remote_copy(
            src_ref=source,
            dst_ref=targets[piece].at[origin, rows],
            send_sem=send_sem.at[index, origin, lane],
            recv_sem=recv_sem.at[index, origin],
            device_id={"own": peer},
            device_id_type=pl.DeviceIdType.MESH,
        )

    def slab_copy(index, step):
        peer = lax.rem(me + step, count)
        return pltpu.make_async_remote_copy(
            src_ref=slabs[index].at[peer],
            dst_ref=landings[index].at[me],
            send_sem=slab_send.at[index, step],
            recv_sem=slab_recv.at[index, step],
            device_id={"own": peer},
            device_id_type=pl.DeviceIdType.MESH,
        )

    def both(index, origin, own, act):
        pl.when(z < far - 1)(lambda: act(copy(index, origin, 0, me + near, own)))
        pl.when(z > 0)(lambda: act(copy(index, origin, 1, me - near, own)))

    def sideways(index, origin, own, act):
        for step in range(1, near):
            act(copy(index, origin, 1 + step, across(step), own))

    def start(item):
        item.start()

    def sent(item):
        item.wait_send()

    def arrived(index, origin):
        copy(index, origin, 0, me, False).wait_recv()

    for index in backs:
        both(index, me, True, start)
    for index in fronts:
        sideways(index, me, True, start)
    for index in backs:
        sideways(index, me, True, start)
    for index in fronts:
        both(index, me, True, start)
    for index in range(exchanged):
        for step in range(1, count):
            slab_copy(index, step).start()
    locals_ = [
        pltpu.make_async_copy(sources[piece], targets[piece].at[me], local_sem.at[piece]) for piece in range(pieces)
    ]
    for index in range(exchanged):
        locals_.append(pltpu.make_async_copy(slabs[index].at[me], landings[index].at[me], local_sem.at[pieces + index]))
    for item in locals_:
        item.start()
    for step in range(1, near):
        for index in fronts:
            arrived(index, across(step))
            both(index, across(step), False, start)

    def hop(distance, direction):
        here = z - direction * distance
        inside = (here >= 0) & (here < far)
        onward = inside & (z + direction >= 0) & (z + direction < far)
        lane = 0 if direction > 0 else 1
        neighbour = me + direction * near
        return here, inside, onward, lane, neighbour

    def travel(act, receive):
        for distance in range(1, far):
            for direction in (1, -1):
                here, inside, onward, lane, neighbour = hop(distance, direction)
                for index in backs:
                    origin = here * near + y
                    if receive:
                        pl.when(inside)(functools.partial(arrived, index, origin))
                    pl.when(onward)(lambda: act(copy(index, origin, lane, neighbour, False)))
                    pl.when(inside)(lambda: sideways(index, origin, False, act))
                for index in fronts:
                    for step in range(near):
                        origin = here * near + lax.rem(y + step, near)
                        if receive:
                            pl.when(inside)(functools.partial(arrived, index, origin))
                        pl.when(onward)(lambda: act(copy(index, origin, lane, neighbour, False)))

    travel(start, True)
    for level in range(far):
        for step in range(1, near):
            for index in backs:
                arrived(index, level * near + lax.rem(y + step, near))
    for index in range(exchanged):
        for step in range(1, count):
            slab_copy(index, step).wait()
    for index in backs + fronts:
        both(index, me, True, sent)
        sideways(index, me, True, sent)
    for step in range(1, near):
        for index in fronts:
            both(index, across(step), False, sent)
    travel(sent, False)
    for item in locals_:
        item.wait()


def relay(count, collective_id, arrays, slabs=()):
    pieces, exchanged = len(arrays), len(slabs)
    parts = sum(a.shape[0] // chunk_rows(a) for a in arrays)
    _, near = plane_split(count)
    shapes = [jax.ShapeDtypeStruct((count,) + a.shape, a.dtype) for a in arrays]
    shapes += [jax.ShapeDtypeStruct(a.shape, a.dtype) for a in slabs]
    return pl.pallas_call(
        functools.partial(relay_kernel, count, pieces, exchanged),
        out_shape=shapes,
        in_specs=[pl.BlockSpec(memory_space=VMEM)] * (pieces + exchanged),
        out_specs=[pl.BlockSpec(memory_space=VMEM)] * (pieces + exchanged),
        scratch_shapes=[
            pltpu.SemaphoreType.DMA((parts, count, near + 1)),
            pltpu.SemaphoreType.DMA((parts, count)),
            pltpu.SemaphoreType.DMA((pieces + exchanged,)),
            pltpu.SemaphoreType.DMA((max(exchanged, 1), count)),
            pltpu.SemaphoreType.DMA((max(exchanged, 1), count)),
        ],
        compiler_params=pltpu.CompilerParams(collective_id=collective_id, has_side_effects=True),
        name="relay",
    )(*arrays, *slabs)


def slide(value, shift_y, shift_x, side):
    cells = value.shape[1]
    lane = lax.broadcasted_iota(jnp.int32, value.shape, 1)
    y = lane // side - shift_y
    x = lax.rem(lane, side) - shift_x
    inside = (y >= 0) & (y < side) & (x >= 0) & (x < side)
    amount = lax.rem(shift_y * side + shift_x + 2 * cells, cells)
    return jnp.where(inside, pltpu.roll(value, amount, axis=1), 0.0)


def pair_kernel(each, side, owner_ref, pairs, corners, boxes, rho):
    base = owner_ref[0] * each
    for turn in range(each):
        first, second = pairs[base + turn, 0], pairs[base + turn, 1]
        dy = corners[second, 0] - corners[first, 0]
        dx = corners[second, 1] - corners[first, 1]
        moved = slide(boxes[second].astype(jnp.float32), dy, dx, side)
        rho[turn] = boxes[first].astype(jnp.float32) * moved


def combine_kernel(side, owner_ref, pairs, corners, boxes, fields, read, phi, out):
    me = owner_ref[0]
    owners, depth, _ = read.shape
    own = phi[...].astype(jnp.float32)
    for owner in range(owners):
        rows = slice(owner * depth, (owner + 1) * depth)
        out[rows, :] = read[owner] * own[rows, :]

    def step(row, carry):
        first, second = pairs[row, 0], pairs[row, 1]
        dy = corners[second, 0] - corners[first, 0]
        dx = corners[second, 1] - corners[first, 1]

        @pl.when(first == me)
        def _():
            moved = slide(boxes[second].astype(jnp.float32), dy, dx, side)
            out[...] -= MIXING * fields[row] * moved

        @pl.when(second == me)
        def _():
            product = fields[row] * boxes[first].astype(jnp.float32)
            out[...] -= MIXING * slide(product, -dy, -dx, side)

        return carry

    lax.fori_loop(0, pairs.shape[0], step, 0)


def local_call(kernel, shape, scalars, arrays, name):
    return pl.pallas_call(
        kernel,
        out_shape=jax.ShapeDtypeStruct(shape, jnp.float32),
        in_specs=[pl.BlockSpec(memory_space=pltpu.SMEM)] * len(scalars)
        + [pl.BlockSpec(memory_space=VMEM)] * len(arrays),
        out_specs=pl.BlockSpec(memory_space=VMEM),
        name=name,
    )(*scalars, *arrays)


def body(owners, groups, orbitals, offsets, pairs, ext_pot):
    owner = lax.axis_index("own")
    _, levels, cells = orbitals.shape
    side = side_of(cells)
    grid = side_of(ext_pot.shape[1])
    depth = levels // owners
    padded = jnp.pad(offsets, ((0, 7), (0, 126)))
    boxes, spread = relay(owners, 0, (orbitals[0], padded))
    corners = spread[:, 0, :2]
    scalars = (owner.reshape(1), pairs, corners)

    planes = lax.dynamic_slice_in_dim(boxes, owner * depth, depth, 1).astype(jnp.float32)
    planes = planes.reshape(owners, depth, side, side)
    along_rows = placer(corners[:, 0], grid, side)
    along_cols = placer(corners[:, 1], grid, side)
    partial = jnp.einsum("izyx,ihx->izyh", planes * planes, along_cols, precision=PRECISE)
    partial = jnp.einsum("igy,izyh->zgh", along_rows, partial, precision=PRECISE)
    partial = partial.reshape(depth, grid * grid)
    density = partial
    for step in range(1, groups):
        density = density + lax.ppermute(partial, "grp", [(g, (g + step) % groups) for g in range(groups)])

    each = pairs.shape[0] // owners
    rho = local_call(
        functools.partial(pair_kernel, each, side), (each, levels, cells), scalars, (boxes,), "pair_density"
    )
    green = green_table(levels, side) * (1.0 / float(8 * levels * cells))
    along_z = cas_table(2 * levels, levels)
    along_y = cas_table(2 * side, side)
    fields = []
    for turn in range(each):
        value = rotate("kz,zc->kc", along_z, rho[turn]).reshape(2 * levels, side, side)
        value = rotate("ky,zyx->zkx", along_y, value)
        value = rotate("kx,zyx->zyk", along_y, value)
        value = lax.optimization_barrier(value * green)
        value = rotate("kx,zyk->zyx", along_y, value)
        value = rotate("ky,zkx->zyx", along_y, value).reshape(2 * levels, cells)
        fields.append(rotate("kz,kc->zc", along_z, value))
    field = jnp.concatenate(fields) if each > 1 else fields[0]

    external = lax.dynamic_slice_in_dim(ext_pot, owner * depth, depth, 0)
    potential = external.astype(jnp.float32) - EXCHANGE_COEF * jnp.cbrt(density)
    potential = potential.reshape(depth, grid, grid)
    read = jnp.einsum("igy,zgh->izyh", along_rows, potential, precision=PRECISE)
    read = jnp.einsum("izyh,ihx->izyx", read, along_cols, precision=PRECISE)
    read = read.reshape(owners, depth, cells)
    every, landed = relay(owners, 1, (field,), (read,))
    every = every.reshape(owners * each, levels, cells)
    gradient = local_call(
        functools.partial(combine_kernel, side),
        (levels, cells),
        scalars,
        (boxes, every, landed, orbitals[0]),
        "combine",
    )
    return gradient[None]


def solution(mesh):
    in_specs = (P(("grp", "own"), None, None), P(("grp", "own"), None), P("grp", None), P())
    out_specs = P(("grp", "own"), None, None)
    run = functools.partial(body, mesh.shape["own"], mesh.shape["grp"])
    return jax.shard_map(run, mesh=mesh, in_specs=in_specs, out_specs=out_specs, check_vma=False)
```

profile of v0, /device:TPU:0, one launch (start us, length us, event | category | flops | bytes accessed | tf_op | source)
XLA Modules:
  0.0 71.8 jit_solution(4953594313291604326)
XLA Ops:
  0.0 0.0 copy-start
  0.0 1.3 %pad.4.refs_1_ = s32[8,128]{1,0:T(8,128)} pad(s32[1,2]{1,0:T(1,128)} %param.5, s32[]{:T(128)} %constant.14.clone.1), padding=0_7x0_126 | pad | bytes 4108 | tf_op jit(solution)/shard_map/jit(_pad)/pad | solution.py:299
  1.3 21.1 %relay.2 = (bf16[8,32,1024]{2,1,0:T(8,128)(2,1)}, s32[8,8,128]{2,1,0:T(8,128)}) custom-call(bf16[32,1024]{1,0:T(8,128)(2,1)} %bitcast.61, s32[8,128]{1,0:T(8,128)} %pad.4.refs_1_), custom_call_target="tpu_custom_call" | custom-call | tf_op jit(solution)/shard_map/relay/pallas_call | solution.py:217
  22.4 0.8 %slice.9 = s32[8,1,2]{2,1,0:T(1,128)S(1)} slice(s32[8,8,128]{2,1,0:T(8,128)} %get-tuple-element.9), slice={[0:8], [0:1], [0:2]} | slice | bytes 128 | tf_op jit(solution)/shard_map/slice | solution.py:301
  23.2 0.1 copy.10
  23.3 0.9 %convert_multiply_fusion = f32[8,4,1024]{2,1,0:T(4,128)S(1)} fusion(bf16[8,32,1024]{2,1,0:T(8,128)(2,1)} %get-tuple-element.10.boxes, s32[]{:T(128)S(6)} %select_n.42), kind=kLoop, calls=%fused_computation.16 | loop fusion | flops 65536 | bytes 196612 | tf_op jit(solution)/shard_map/mul | solution.py:308
  24.2 0.2 mul.94
  24.4 0.4 fusion.1
  24.8 0.6 convolution_bitcast_fusion.3
  25.4 0.1 copy.14
  25.5 0.1 reshape.88
  25.6 0.1 collective-permute-start.2
  25.7 1.6 %collective-permute-start.1 = (f32[4,4096]{1,0:T(4,128)S(1)}, f32[4,4096]{1,0:T(4,128)S(1)}, u32[]{:S(2)}, u32[]{:S(2)}) collective-permute-start(f32[4,4096]{1,0:T(4,128)S(1)} %reshape.88), channel_id=1, source_target_pairs={{0,16},{8,24},{16,0},{24,8},{1,17},{9,25},{17,1},{25,9},{2,18},{10... | collective-permute-start | bytes 196616 | tf_op jit(solution)/shard_map/ppermute | solution.py:313
  27.3 0.2 collective-permute-start
  27.4 0.7 copy.16.corners
  28.1 0.0 copy-done
  28.1 0.7 copy.15.pairs
  28.8 1.8 %pair_density.1 = f32[1,32,1024]{2,1,0:T(8,128)} custom-call(s32[1]{0:T(128)} %bitcast.owner_ref, s32[8,2]{1,0:T(8,128)} %copy.15.pairs, s32[8,2]{1,0:T(8,128)} %copy.16.corners, bf16[8,32,1024]{2,1,0:T(8,128)(2,1)} %get-tuple-element.10.boxes), custom_call_target="tpu_custom_call" | custom-call | tf_op jit(solution)/shard_map/pair_density/pallas_call | solution.py:283
  30.6 1.1 %dot_general.35 = f32[32,32,32]{1,0,2:T(8,128)S(1)} reshape(f32[1024,32]{0,1:T(8,128)} %bitcast.60) | data formatting | bytes 262144 | tf_op jit(solution)/shard_map/kz,zc->kc/dot_general | solution.py:45
  31.7 0.8 %fusion.3 = f32[64,32,32]{0,2,1:T(8,128)S(1)} fusion(f32[32,32,32]{1,0,2:T(8,128)S(1)} %dot_general.35), kind=kOutput, calls=%fused_computation.8 | convolution fusion | flops 12613632 | bytes 393216 | tf_op jit(solution)/shard_map/kz,zc->kc/dot_general | solution.py:45
  32.5 0.9 %copy.18 = f32[64,32,32]{2,1,0:T(8,128)S(1)} copy(f32[64,32,32]{0,2,1:T(8,128)S(1)} %fusion.3) | data formatting | bytes 524288 | tf_op jit(solution)/shard_map/kz,zc->kc/dot_general | solution.py:45
  33.4 1.0 %convolution_bitcast_fusion = f32[64,64,32]{1,2,0:T(8,128)S(1)} fusion(f32[64,32,32]{2,1,0:T(8,128)S(1)} %copy.18), kind=kOutput, calls=%fused_computation.1 | convolution fusion | flops 25196544 | bytes 786432 | tf_op jit(solution)/shard_map/ky,zyx->zkx/dot_general | solution.py:45
  34.4 0.1 broadcast_add_fusion
  34.5 2.3 %multiply_multiply_fusion = f32[64,64,64]{2,1,0:T(8,128)S(1)} fusion(f32[64,64,32]{1,2,0:T(8,128)S(1)} %convolution_bitcast_fusion, f32[64]{0:T(128)S(1)} %fusion.33, f32[64,64]{1,0:T(8,128)S(1)} %broadcast_add_fusion), kind=kOutput, calls=%fused_computation | convolution fusion | flops 51673088 | bytes 1589504 | tf_op jit(solution)/shard_map/kx,zyx->zyk/dot_general | solution.py:45
  36.8 3.0 %fusion.22 = f32[64,64,32]{1,2,0:T(8,128)S(1)} fusion(f32[64,64,64]{2,1,0:T(8,128)S(1)} %multiply_multiply_fusion), kind=kOutput, calls=%fused_computation.30 | convolution fusion | flops 50362368 | bytes 1572864 | tf_op jit(solution)/shard_map/kx,zyk->zyx/dot_general | solution.py:45
  39.8 1.8 %convolution_bitcast_fusion.2 = f32[64,32,32]{0,1,2:T(8,128)S(1)} fusion(f32[64,64,32]{1,2,0:T(8,128)S(1)} %fusion.22), kind=kOutput, calls=%fused_computation.3 | convolution fusion | flops 25196544 | bytes 786432 | tf_op jit(solution)/shard_map/ky,zkx->zyx/dot_general | solution.py:45
  41.6 0.3 copy.13
  41.9 1.1 %fusion.30.refs_0_ = f32[32,1024]{1,0:T(8,128)} fusion(f32[64,1024]{0,1:T(8,128)S(1)} %bitcast.59), kind=kOutput, calls=%fused_computation.40 | convolution fusion | flops 12613632 | bytes 393216 | tf_op jit(solution)/shard_map/kz,kc->zc/dot_general | solution.py:45
  43.0 0.0 collective-permute-done.2
  43.0 0.0 collective-permute-done.1
  43.0 0.0 collective-permute-done
  43.0 1.0 %multiply_subtract_fusion = f32[4,4096]{1,0:T(4,128)S(1)} fusion(f32[4,4096]{1,0:T(4,128)S(1)} %collective-permute-done.2, f32[4,4096]{1,0:T(4,128)S(1)} %collective-permute-done.1, f32[4,4096]{1,0:T(4,128)S(1)} %reshape.88, f32[4,4096]{1,0:T(4,128)S(1)} %collective-permute-done, bf16[32,4096]{1,0:T(8,128)(2,1)} %param.7, s32[]{:T(128)S(6)} %select_n.42), kind=kLoop, calls=%fused_computation.18 | loop fusion | flops 98304 | bytes 360452 | tf_op jit(solution)/shard_map/sub | solution.py:334
  44.0 0.1 reshape.95
  44.1 0.4 convolution_bitcast_fusion.1
  44.5 0.4 fusion.10
  45.0 0.9 %reshape.90.refs_1_ = f32[8,4,1024]{2,1,0:T(4,128)} reshape(f32[8,4,32,32]{3,2,1,0:T(8,128)S(1)} %fusion.10) | data formatting | bytes 262144 | tf_op jit(solution)/shard_map/reshape | solution.py:338
  45.9 23.4 %relay.3 = (f32[8,32,1024]{2,1,0:T(8,128)}, f32[8,4,1024]{2,1,0:T(4,128)}) custom-call(f32[32,1024]{1,0:T(8,128)} %fusion.30.refs_0_, f32[8,4,1024]{2,1,0:T(4,128)} %reshape.90.refs_1_), custom_call_target="tpu_custom_call" | custom-call | tf_op jit(solution)/shard_map/relay/pallas_call | solution.py:217
  69.3 2.5 %combine.1 = f32[32,1024]{1,0:T(8,128)} custom-call(s32[1]{0:T(128)} %bitcast.owner_ref, s32[8,2]{1,0:T(8,128)} %copy.15.pairs, s32[8,2]{1,0:T(8,128)} %copy.16.corners, bf16[8,32,1024]{2,1,0:T(8,128)(2,1)} %get-tuple-element.10.boxes, f32[8,32,1024]{2,1,0:T(8,128)} %get-tuple-element.11.fields, f32[8,4,1024]{2,1,0:T(4,128)} %get-tuple-element.12.read, ...), custom_call_target="tpu_custom_call" | custom-call | tf_op jit(solution)/shard_map/combine/pallas_call | solution.py:283
  (2 shorter events, 0.0 us)
Async XLA Ops:
  0.0 28.1 %copy-start = (s32[8,2]{0,1:T(2,128)S(1)}, s32[8,2]{0,1:T(2,128)}, u32[]{:S(2)}) copy-start(s32[8,2]{0,1:T(2,128)} %param.6) | copy-start | bytes 196
  25.6 17.4 %collective-permute-start.2 = (f32[4,4096]{1,0:T(4,128)S(1)}, f32[4,4096]{1,0:T(4,128)S(1)}, u32[]{:S(2)}, u32[]{:S(2)}) collective-permute-start(f32[4,4096]{1,0:T(4,128)S(1)} %reshape.88), channel_id=1, source_target_pairs={{0,24},{8,0},{16,8},{24,16},{1,25},{9,1},{17,9},{25,17},{2,26},{10... | collective-permute-start | bytes 196616 | tf_op jit(solution)/shard_map/ppermute | solution.py:313
  25.7 17.3 %collective-permute-start.1 = (f32[4,4096]{1,0:T(4,128)S(1)}, f32[4,4096]{1,0:T(4,128)S(1)}, u32[]{:S(2)}, u32[]{:S(2)}) collective-permute-start(f32[4,4096]{1,0:T(4,128)S(1)} %reshape.88), channel_id=1, source_target_pairs={{0,16},{8,24},{16,0},{24,8},{1,17},{9,25},{17,1},{25,9},{2,18},{10... | collective-permute-start | bytes 196616 | tf_op jit(solution)/shard_map/ppermute | solution.py:313
  27.3 15.7 %collective-permute-start = (f32[4,4096]{1,0:T(4,128)S(1)}, f32[4,4096]{1,0:T(4,128)S(1)}, u32[]{:S(2)}, u32[]{:S(2)}) collective-permute-start(f32[4,4096]{1,0:T(4,128)S(1)} %reshape.88), channel_id=1, source_target_pairs={{0,8},{8,16},{16,24},{24,0},{1,9},{9,17},{17,25},{25,1},{2,10},{10... | collective-permute-start | bytes 196616 | tf_op jit(solution)/shard_map/ppermute | solution.py:313
where the time goes:
time: 72.2 us; the launch traced here: 71.8 us
  Pallas kernels  48.8 us (68%)
  matrix products  11.8 us (16%)
  local copies, waits for them, and re-layouts  7.18 us (10%)
  other arithmetic  2.01 us (3%)
  starting transfers between devices  1.76 us (2%)
    pallas_call x2, Pallas kernels, relay(): pl.pallas_call(functools.partial(relay_kernel, count, pieces, exchanged),...  44.5 us
    dot_general x6, matrix products, rotate(): jnp.einsum(pattern, matrix, operand, precision=SPLIT, preferred_element_t...  9.97 us
    pallas_call x2, Pallas kernels, local_call(): pl.pallas_call(kernel, out_shape=jax.ShapeDtypeStruct(shape, jnp.float32)...  4.32 us
    dot_general x2, local copies, waits for them, and re-layouts, rotate(): jnp.einsum(pattern, matrix, operand, precision=SPLIT, preferred_element_t...  2 us
    ppermute x3, starting transfers between devices, body(): lax.ppermute(partial, 'grp', [(g, (g + step) % groups) for g in range(gro...  1.76 us
  transfers between devices with their start and end apart: 3, of which 0 were waited for; matrix products, arithmetic and copies ran while one was open for 19% of the time, Pallas kernels for 3%

commit v1 on v0

v1 whole, which is shorter than its diff:
```python
import functools
import math

import jax
import jax.numpy as jnp
import ml_dtypes
import numpy as np
from jax import lax
from jax.experimental import pallas as pl
from jax.experimental.pallas import tpu as pltpu
from jax.sharding import PartitionSpec as P

SCREEN = 0.0025
MIXING = 0.25
EXCHANGE_COEF = (3.0 / math.pi) ** (1.0 / 3.0)
LANES = 128
TILE = 8
CHUNK = 16
VMEM = pltpu.VMEM
MESH = pl.DeviceIdType.MESH
F32 = jnp.float32
BF16 = jnp.bfloat16


class Sizes:
    def __init__(self, owners, groups, levels, cells, grid_cells, pairs):
        self.owners, self.groups, self.levels, self.cells, self.pairs = owners, groups, levels, cells, pairs
        self.side, self.grid = math.isqrt(cells), math.isqrt(grid_cells)
        self.depth = levels // owners
        self.each = pairs // owners
        self.rows = cells // LANES
        self.per = LANES // self.side
        self.slab = self.depth * self.rows
        self.grid_rows = grid_cells // LANES
        self.halves = self.per * self.grid // LANES
        self.waves = 2 * levels
        self.turns = 2 * self.side // self.per
        self.wide = self.per * 2 * self.side
        self.block = self.turns * CHUNK
        self.chunks = self.waves // CHUNK


def halves_of(table):
    high = table.astype(ml_dtypes.bfloat16)
    low = (table - high.astype(np.float64)).astype(ml_dtypes.bfloat16)
    return high, low


def cas(angle):
    return np.cos(angle) + np.sin(angle)


def tables(n):
    side, per, levels = n.side, n.per, n.levels
    along_z = cas(2.0 * np.pi / n.waves * np.outer(np.arange(n.waves), np.arange(levels)))
    high, low = halves_of(along_z)
    to_waves = np.concatenate([high, high, low], axis=1)
    high, low = halves_of(along_z.T)
    from_waves = np.concatenate([high, high, low], axis=1)
    along_x = cas(np.pi / side * np.outer(np.arange(side), np.arange(2 * side)))
    phase = 2.0 * np.pi / per * np.outer(np.arange(per), np.arange(per))
    lane = np.concatenate(
        [np.einsum("yh,xk->yxhk", wave(phase), along_x).reshape(LANES, n.wide) for wave in (np.cos, np.sin)]
    )
    lane = np.stack(halves_of(lane))
    lane_back = np.ascontiguousarray(np.swapaxes(lane, 1, 2))
    angle = np.pi / side * np.outer(np.arange(n.turns), np.arange(LANES) // side)
    twiddle = np.concatenate([cas(angle), cas(-angle)]).astype(np.float32)

    def squares(length):
        m = np.arange(length)
        return (2.0 * np.pi / length * np.where(m < length // 2, m, m - length)) ** 2

    z = squares(n.waves).reshape(n.chunks, 1, CHUNK, 1, 1)
    y = squares(2 * side).reshape(per, n.turns).T.reshape(1, n.turns, 1, per, 1)
    x = squares(2 * side).reshape(1, 1, 1, 1, 2 * side)
    green = 4.0 * np.pi / (z + y + x + SCREEN) / (n.waves * 4.0 * side * side)
    green = green.reshape(n.chunks * n.block, n.wide).astype(np.float32)
    spread = np.zeros((LANES, n.halves * LANES), ml_dtypes.bfloat16)
    for cell in range(LANES):
        spread[cell, cell // side * n.grid + cell % side] = 1
    gather = np.ascontiguousarray(spread.T)
    return to_waves, from_waves, lane, lane_back, twiddle, green, spread, gather


def split(value):
    high = value.astype(BF16)
    return high, (value - high.astype(F32)).astype(BF16)


def dot(left, right):
    return jnp.dot(left, right, preferred_element_type=F32)


def thrice(high, low, matrix):
    return dot(high, matrix[0]) + dot(low, matrix[0]) + dot(high, matrix[1])


def flat_roll(value, amount):
    carried = lax.rem(amount, LANES)
    down = amount // LANES
    rows = value.shape[1]
    turned = pltpu.roll(value, carried, axis=2)
    here = pltpu.roll(turned, down, axis=1)
    above = pltpu.roll(turned, lax.rem(down + 1, rows), axis=1)
    lane = lax.broadcasted_iota(jnp.int32, value.shape, 2)
    return jnp.where(lane >= carried, here, above)


def slide(n, value, shift_y, shift_x):
    shape = value.shape
    value = value.reshape(shape[0] // n.rows, n.rows, LANES)
    row = lax.broadcasted_iota(jnp.int32, value.shape, 1)
    lane = lax.broadcasted_iota(jnp.int32, value.shape, 2)
    y = row * n.per + lane // n.side - shift_y
    x = lax.rem(lane, n.side) - shift_x
    inside = (y >= 0) & (y < n.side) & (x >= 0) & (x < n.side)
    amount = lax.rem(shift_y * n.side + shift_x + 2 * n.cells, n.cells)
    return jnp.where(inside, flat_roll(value, amount), 0.0).reshape(shape)


def wave_sums(n, values):
    top, half = n.turns // 2, n.turns // 4
    cosines, sines = [None] * (top + 1), [None] * (top + 1)
    for q in range(half + 1):
        sums = []
        for wave in (math.cos, math.sin):
            for parity in (0, 1):
                total = None
                for s in range(parity, n.rows, 2):
                    factor = wave(2.0 * math.pi * q * s / n.turns)
                    total = weighted(total, factor, values[s])
                sums.append(total)
        even_cos, odd_cos, even_sin, odd_sin = sums
        cosines[q] = plus(even_cos, odd_cos)
        cosines[top - q] = minus(even_cos, odd_cos)
        sines[q] = plus(even_sin, odd_sin)
        sines[top - q] = minus(odd_sin, even_sin)
    return cosines, sines


def weighted(total, factor, value):
    if value is None or abs(factor) < 1e-12:
        return total
    if abs(abs(factor) - 1.0) < 1e-12:
        if factor > 0:
            return value if total is None else total + value
        return -value if total is None else total - value
    term = factor * value
    return term if total is None else total + term


def plus(left, right):
    if left is None or right is None:
        return right if left is None else left
    return left + right


def minus(left, right):
    if right is None:
        return left
    return -right if left is None else left - right


def cell_sums(n, cosines, sines):
    top, half = n.turns // 2, n.turns // 4
    values = []
    folded = {}
    for q in range(half + 1):
        if q == top - q:
            folded[q] = (cosines[q], cosines[q], sines[q], sines[q])
        else:
            c, d, s, t = cosines[q], cosines[top - q], sines[q], sines[top - q]
            folded[q] = (plus(c, d), minus(c, d), minus(s, t), plus(s, t))
    for s in range(n.rows):
        total = None
        odd = s % 2
        for q in range(half + 1):
            angle = 2.0 * math.pi * q * s / n.turns
            total = weighted(total, math.cos(angle), folded[q][odd])
            total = weighted(total, math.sin(angle), folded[q][2 + odd])
        values.append(total)
    return values


def solve(n, rho, stack, waves, high_ref, low_ref, back, spectrum, to_waves, from_waves, lane, lane_back, twiddle, green):
    levels = n.levels
    for s in range(n.rows):
        columns = slice(s * LANES, (s + 1) * LANES)
        high, low = split(rho[pl.ds(s, levels, stride=n.rows), :])
        stack[0:levels, columns] = high
        stack[levels : 2 * levels, columns] = low
        stack[2 * levels : 3 * levels, columns] = high
    waves[...] = dot(to_waves[...], stack[...])
    top = n.turns // 2
    for chunk in range(n.chunks):
        band = slice(chunk * CHUNK, (chunk + 1) * CHUNK)
        cosines, sines = wave_sums(n, [waves[band, s * LANES : (s + 1) * LANES] for s in range(n.rows)])
        for q in range(n.turns):
            same = q <= top
            a = cosines[q if same else n.turns - q]
            b = sines[q if same else n.turns - q]
            ahead = twiddle[q : q + 1, :]
            behind = twiddle[n.turns + q : n.turns + q + 1, :]
            u, w = ahead * a, behind * a
            if b is not None and q % top:
                u = u + behind * b if same else u - behind * b
                w = w - ahead * b if same else w + ahead * b
            rows = slice(chunk * n.block + q * CHUNK, chunk * n.block + (q + 1) * CHUNK)
            for index, part in enumerate((u, w)):
                columns = slice(index * LANES, (index + 1) * LANES)
                high_ref[rows, columns], low_ref[rows, columns] = split(part)
    for chunk in range(n.chunks):
        rows = slice(chunk * n.block, (chunk + 1) * n.block)
        value = thrice(high_ref[rows, :], low_ref[rows, :], lane) * green[rows, :]
        high, low = split(value)
        back[rows, :] = thrice(high, low, lane_back)
    for chunk in range(n.chunks):
        cosines, sines = [None] * (top + 1), [None] * (top + 1)
        for q in range(n.turns):
            rows = slice(chunk * n.block + q * CHUNK, chunk * n.block + (q + 1) * CHUNK)
            u, w = back[rows, 0:LANES], back[rows, LANES : 2 * LANES]
            ahead = twiddle[q : q + 1, :]
            behind = twiddle[n.turns + q : n.turns + q + 1, :]
            a = ahead * u + behind * w
            if q <= top:
                cosines[q] = a
            else:
                cosines[n.turns - q] = cosines[n.turns - q] + a
            if q % top:
                b = behind * u - ahead * w
                sines[q if q <= top else n.turns - q] = (
                    b if q <= top else sines[n.turns - q] - b
                )
        values = cell_sums(n, cosines, sines)
        for s in range(n.rows):
            columns = slice(s * LANES, (s + 1) * LANES)
            high, low = split(values[s])
            for place, part in enumerate((high, low, high)):
                start = place * n.waves + chunk * CHUNK
                spectrum[start : start + CHUNK, columns] = part
    return dot(from_waves[...], spectrum[...])


def kernel(n, pairs, offsets, orbital, external, *refs):
    table_refs, refs = refs[:8], refs[8:]
    out, refs = refs[0], refs[1:]
    table_dst, refs = refs[:8], refs[8:]
    (own_box, flat, box_send, box_land, place_send, place_land, corner, near, moved, rho_send, rho_land) = refs[:11]
    (field_send, field_land, ext_block, ext_flat, dens_grid, dens_send, dens_land, level, read_in, read) = refs[11:21]
    (grad_send, stack, waves, high_ref, low_ref, back, spectrum) = refs[21:28]
    local_sem, own_send, own_recv, grp_send, grp_recv = refs[28:]
    to_waves, from_waves, lane, lane_back, twiddle, green, spread, gather = table_dst
    owners, groups, depth, slab = n.owners, n.groups, n.depth, n.slab
    me, team = lax.axis_index("own"), lax.axis_index("grp")

    own_in = pltpu.make_async_copy(orbital, own_box, local_sem.at[0])
    own_in.start()
    first_level = pl.multiple_of(me * depth // TILE * TILE, TILE)
    taken = ext_block.shape[0]
    ext_in = pltpu.make_async_copy(external.at[pl.ds(first_level, taken)], ext_block, local_sem.at[1])
    ext_in.start()
    table_in = [
        pltpu.make_async_copy(source, target, local_sem.at[2 + i])
        for i, (source, target) in enumerate(zip(table_refs, table_dst))
    ]
    for item in table_in:
        item.start()
    barrier = pltpu.get_barrier_semaphore()
    for step in range(1, owners):
        peer = lax.rem(me + step, owners)
        pl.semaphore_signal(barrier, inc=1, device_id={"own": peer}, device_id_type=MESH)
    for step in range(1, groups):
        peer = lax.rem(team + step, groups)
        pl.semaphore_signal(barrier, inc=1, device_id={"grp": peer}, device_id_type=MESH)

    row_index = lax.broadcasted_iota(jnp.int32, place_send.shape, 0)
    place_send[...] = jnp.where(row_index == 0, offsets[0, 0], offsets[0, 1])
    own_in.wait()
    for s in range(n.rows):
        flat[pl.ds(s, n.levels, stride=n.rows), :] = own_box[:, s * LANES : (s + 1) * LANES].astype(F32)
    for owner in range(owners):
        box_send[owner] = flat[owner * slab : (owner + 1) * slab, :].astype(BF16)
    pl.semaphore_wait(barrier, owners + groups - 2)

    def to_owner(phase, step, source, target):
        peer = lax.rem(me + step, owners)
        return pltpu.make_async_remote_copy(
            src_ref=source,
            dst_ref=target,
            send_sem=own_send.at[phase, step],
            recv_sem=own_recv.at[phase, step],
            device_id={"own": peer},
            device_id_type=MESH,
        )

    def part(ref, index, size):
        return ref.at[pl.ds(pl.multiple_of(index * size, size), size)]

    sent = []
    boxes_in = []
    for step in range(1, owners):
        peer = lax.rem(me + step, owners)
        boxes_in.append(to_owner(0, step, place_send, place_land.at[me]))
        boxes_in.append(to_owner(1, step, box_send.at[peer], box_land.at[me]))
        boxes_in[-2].start()
        boxes_in[-1].start()
    sent += boxes_in
    place_land[me] = place_send[...]
    box_land[me] = box_send[me]
    for item in boxes_in:
        item.wait_recv()
    for owner in range(owners):
        corner[owner, 0] = place_land[owner, 0, 0]
        corner[owner, 1] = place_land[owner, 1, 0]

    def shift_of(row):
        first, second = pairs[row, 0], pairs[row, 1]
        return corner[second, 0] - corner[first, 0], corner[second, 1] - corner[first, 1]

    rho_in = []
    bundle = n.each * slab
    for step in [*range(1, owners), 0]:
        peer = lax.rem(me + step, owners)
        for turn in range(n.each):
            row = peer * n.each + turn
            dy, dx = shift_of(row)
            a = box_land[pairs[row, 0]].astype(F32)
            b = slide(n, box_land[pairs[row, 1]].astype(F32), dy, dx)
            near[row] = a
            moved[row] = b
            if step:
                rho_send[peer, turn] = a * b
            else:
                rho_land[turn, pl.ds(pl.multiple_of(me * slab, slab), slab), :] = a * b
        if step:
            for turn in range(n.each):
                target = rho_land.at[turn, pl.ds(pl.multiple_of(me * slab, slab), slab)]
                rho_in.append(to_owner(2 + turn, step, rho_send.at[peer, turn], target))
                rho_in[-1].start()
    sent += rho_in

    for item in table_in:
        item.wait()
    grid_shape = (depth, n.grid_rows, LANES)
    for owner in range(owners):
        value = box_land[owner].astype(F32)
        high, low = split(value * value)
        wide = dot(high, spread[...]) + dot(low, spread[...])
        for z in range(depth):
            start = z * n.grid_rows
            for half in range(n.halves):
                rows = pl.ds(start + half, n.rows, stride=n.halves)
                dens_grid[owner, rows, :] = wide[z * n.rows : (z + 1) * n.rows, half * LANES : (half + 1) * LANES]
            rest = n.grid_rows - n.rows * n.halves
            dens_grid[owner, start + n.rows * n.halves : start + n.grid_rows, :] = jnp.zeros((rest, LANES), F32)
    total = jnp.zeros(grid_shape, F32)
    for owner in range(owners):
        amount = corner[owner, 0] * n.grid + corner[owner, 1]
        total = total + flat_roll(dens_grid[owner].reshape(grid_shape), amount)
    dens_send[...] = total.reshape(dens_send.shape)
    dens_in = []
    for step in range(1, groups):
        dens_in.append(
            pltpu.make_async_remote_copy(
                src_ref=dens_send,
                dst_ref=dens_land.at[step],
                send_sem=grp_send.at[step],
                recv_sem=grp_recv.at[step],
                device_id={"grp": lax.rem(team + step, groups)},
                device_id_type=MESH,
            )
        )
        dens_in[-1].start()
    sent += dens_in

    for item in rho_in:
        item.wait_recv()
    field_in = []
    for turn in range(n.each):
        field = solve(
            n, rho_land.at[turn], stack, waves, high_ref, low_ref, back, spectrum,
            to_waves, from_waves, lane, lane_back, twiddle, green,
        )
        for s in range(n.rows):
            field_send[turn, pl.ds(s, n.levels, stride=n.rows), :] = field[:, s * LANES : (s + 1) * LANES]
        for step in range(1, owners):
            peer = lax.rem(me + step, owners)
            source = field_send.at[turn, pl.ds(pl.multiple_of(peer * slab, slab), slab)]
            field_in.append(to_owner(2 + n.each + turn, step, source, field_land.at[me * n.each + turn]))
            field_in[-1].start()
        field_land[me * n.each + turn] = field_send[turn, pl.ds(pl.multiple_of(me * slab, slab), slab), :]
    sent += field_in

    ext_in.wait()
    ext_values = ext_block[...].astype(F32)
    for k in range(n.grid_rows):
        ext_flat[pl.ds(k, taken, stride=n.grid_rows), :] = ext_values[:, k * LANES : (k + 1) * LANES]
    for item in dens_in:
        item.wait_recv()
    density = dens_send[...]
    for step in range(1, groups):
        density = density + dens_land[step]
    start = pl.multiple_of((me * depth - first_level) * n.grid_rows, n.grid_rows)
    outside = ext_flat[pl.ds(start, depth * n.grid_rows), :]
    safe = jnp.where(density > 0.0, density, 1.0)
    root = jnp.exp(jnp.log(safe) * (1.0 / 3.0))
    root = root - (root - safe / (root * root)) * (1.0 / 3.0)
    level[...] = outside - EXCHANGE_COEF * jnp.where(density > 0.0, root, 0.0)
    whole = n.grid_rows * LANES
    for owner in range(owners):
        amount = lax.rem(whole - corner[owner, 0] * n.grid - corner[owner, 1], whole)
        turned = flat_roll(level[...].reshape(grid_shape), amount)
        read_in[owner] = turned.reshape(read_in.shape[1:])
        parts = []
        for z in range(depth):
            pieces = [
                read_in[owner, pl.ds(z * n.grid_rows + half, n.rows, stride=n.halves), :] for half in range(n.halves)
            ]
            parts.append(jnp.concatenate(pieces, axis=1) if n.halves > 1 else pieces[0])
        value = jnp.concatenate(parts, axis=0) if depth > 1 else parts[0]
        high, low = split(value)
        read[owner] = (dot(high, gather[...]) + dot(low, gather[...])) * box_land[owner].astype(F32)

    for item in field_in:
        item.wait_recv()
    for row in range(n.pairs):
        dy, dx = shift_of(row)
        field = field_land[row] * MIXING
        moved[row] = field * moved[row]
        near[row] = slide(n, field * near[row], -dy, -dx)
    grad_in = []
    for step in [*range(1, owners), 0]:
        peer = lax.rem(me + step, owners)
        total = read[peer]
        for row in range(n.pairs):
            total = total - jnp.where(pairs[row, 0] == peer, moved[row], 0.0)
            total = total - jnp.where(pairs[row, 1] == peer, near[row], 0.0)
        if step:
            grad_send[peer] = total
            grad_in.append(to_owner(2 + 2 * n.each, step, grad_send.at[peer], out.at[me]))
            grad_in[-1].start()
        else:
            out[me] = total
    sent += grad_in
    for item in grad_in:
        item.wait_recv()
    for item in sent:
        item.wait_send()


def relayout_kernel(n, slabs, out):
    for owner in range(n.owners):
        for z in range(n.depth):
            rows = slabs[owner, z * n.rows : (z + 1) * n.rows, :]
            for s in range(n.rows):
                row = owner * n.depth + z
                out[row : row + 1, s * LANES : (s + 1) * LANES] = rows[s : s + 1, :]


def body(owners, groups, orbitals, offsets, pairs, ext_pot):
    _, levels, cells = orbitals.shape
    n = Sizes(owners, groups, levels, cells, ext_pot.shape[1], pairs.shape[0])
    consts = tables(n)
    taken = max(n.depth, TILE)
    slabs = (n.owners, n.slab, LANES)
    flat_rows = levels * n.rows
    scratch = [VMEM(c.shape, c.dtype) for c in consts]
    scratch += [
        VMEM((levels, cells), BF16),
        VMEM((flat_rows, LANES), F32),
        VMEM(slabs, BF16),
        VMEM(slabs, BF16),
        VMEM((TILE, LANES), jnp.int32),
        VMEM((owners, TILE, LANES), jnp.int32),
        pltpu.SMEM((owners, 2), jnp.int32),
        VMEM((n.pairs, n.slab, LANES), F32),
        VMEM((n.pairs, n.slab, LANES), F32),
        VMEM((owners, n.each, n.slab, LANES), F32),
        VMEM((n.each, flat_rows, LANES), F32),
        VMEM((n.each, flat_rows, LANES), F32),
        VMEM((n.pairs, n.slab, LANES), F32),
        VMEM((taken, ext_pot.shape[1]), BF16),
        VMEM((taken * n.grid_rows, LANES), F32),
        VMEM((owners, n.depth * n.grid_rows, LANES), F32),
        VMEM((n.depth * n.grid_rows, LANES), F32),
        VMEM((groups, n.depth * n.grid_rows, LANES), F32),
        VMEM((n.depth * n.grid_rows, LANES), F32),
        VMEM((owners, n.depth * n.grid_rows, LANES), F32),
        VMEM(slabs, F32),
        VMEM(slabs, F32),
        VMEM((3 * levels, cells), BF16),
        VMEM((n.waves, cells), F32),
        VMEM((n.chunks * n.block, 2 * LANES), BF16),
        VMEM((n.chunks * n.block, 2 * LANES), BF16),
        VMEM((n.chunks * n.block, 2 * LANES), F32),
        VMEM((3 * n.waves, cells), BF16),
        pltpu.SemaphoreType.DMA((2 + len(consts),)),
        pltpu.SemaphoreType.DMA((3 + 2 * n.each, owners)),
        pltpu.SemaphoreType.DMA((3 + 2 * n.each, owners)),
        pltpu.SemaphoreType.DMA((groups,)),
        pltpu.SemaphoreType.DMA((groups,)),
    ]
    smem = pl.BlockSpec(memory_space=pltpu.SMEM)
    anywhere = pl.BlockSpec(memory_space=pl.ANY)
    slab_out = pl.pallas_call(
        functools.partial(kernel, n),
        out_shape=jax.ShapeDtypeStruct(slabs, F32),
        in_specs=[smem, smem] + [anywhere] * (2 + len(consts)),
        out_specs=pl.BlockSpec(memory_space=VMEM),
        scratch_shapes=scratch,
        compiler_params=pltpu.CompilerParams(collective_id=0, has_side_effects=True),
        name="gradient",
    )(pairs, offsets, orbitals[0], ext_pot, *consts)
    gradient = pl.pallas_call(
        functools.partial(relayout_kernel, n),
        out_shape=jax.ShapeDtypeStruct((levels, cells), F32),
        in_specs=[pl.BlockSpec(memory_space=VMEM)],
        out_specs=pl.BlockSpec(memory_space=VMEM),
        name="relayout",
    )(slab_out)
    return gradient[None]


def solution(mesh):
    in_specs = (P(("grp", "own"), None, None), P(("grp", "own"), None), P("grp", None), P())
    out_specs = P(("grp", "own"), None, None)
    run = functools.partial(body, mesh.shape["own"], mesh.shape["grp"])
    return jax.shard_map(run, mesh=mesh, in_specs=in_specs, out_specs=out_specs, check_vma=False)
```

time: 72.2 us -> 31.6 us (0.44)
  Pallas kernels: 48.8 us -> 30.1 us
  matrix products: 11.8 us -> 0 us
  local copies, waits for them, and re-layouts: 7.18 us -> 1.35 us
  other arithmetic: 2.01 us -> 0 us
  starting transfers between devices: 1.76 us -> 0 us
    pallas_call x4 -> x2, Pallas kernels: 48.8 us -> 30.1 us  [the longest x1 28.4 us: body(): pl.pallas_call(functools.partial(kernel, n), out_shape=jax.ShapeDtypeStru...]
    dot_general x10 -> x0, matrix products: 11.8 us -> none  [the longest x6 9.97 us: rotate(): jnp.einsum(pattern, matrix, operand, precision=SPLIT, preferred_element_t...]
    dot_general x2 -> x0, local copies, waits for them, and re-layouts: 2 us -> none  [rotate(): jnp.einsum(pattern, matrix, operand, precision=SPLIT, preferred_element_t...]
    ppermute x3 -> x0, starting transfers between devices: 1.76 us -> none  [body(): lax.ppermute(partial, 'grp', [(g, (g + step) % groups) for g in range(gro...]
    pad x1 -> x0, local copies, waits for them, and re-layouts: 1.26 us -> none  [body(): padded = jnp.pad(offsets, ((0, 7), (0, 126)))]
    reshape x3 -> x0, local copies, waits for them, and re-layouts: 1.14 us -> none  [the longest x1 0.91 us: body(): read = read.reshape(owners, depth, cells)]
    sub x1 -> x0, other arithmetic: 0.99 us -> none  [body(): potential = external.astype(jnp.float32) - EXCHANGE_COEF * jnp.cbrt(density)]
    mul x2 -> x0, other arithmetic: 0.95 us -> none  [the longest x1 0.94 us: body(): planes * planes]
  transfers between devices with their start and end apart: 3 -> 0, of which waited for: 0 -> 0; matrix products, arithmetic and copies ran while one was open for 19% -> 0% of each run, Pallas kernels for 3% -> 0%
where the time goes in v1:
time: 31.6 us; the launch traced here: 31.4 us
  Pallas kernels  30.1 us (95%)
  local copies, waits for them, and re-layouts  1.35 us (4%)
    pallas_call x1, Pallas kernels, body(): pl.pallas_call(functools.partial(kernel, n), out_shape=jax.ShapeDtypeStru...  28.4 us
    pallas_call x1, Pallas kernels, body(): pl.pallas_call(functools.partial(relayout_kernel, n), out_shape=jax.Shape...  1.63 us
    unnamed x3, local copies, waits for them, and re-layouts  1.35 us

profile of v1, /device:TPU:0, one launch (start us, length us, event | category | flops | bytes accessed | tf_op | source)
XLA Modules:
  0.0 31.4 jit_solution(8804292484251125949)
XLA Ops:
  0.0 0.0 copy-start
  0.0 0.7 %copy-done = s32[8,2]{0,1:T(2,128)S(1)} copy-done((s32[8,2]{0,1:T(2,128)S(1)}, s32[8,2]{0,1:T(2,128)}, u32[]{:S(2)}) %copy-start) | copy-done | bytes 88
  0.7 0.7 %copy.13.pairs = s32[8,2]{1,0:T(8,128)} copy(s32[8,2]{0,1:T(2,128)S(1)} %copy-done) | data formatting | bytes 128 | tf_op args[2]
  1.4 28.4 %gradient.1.slabs = f32[8,32,128]{2,1,0:T(8,128)} custom-call(s32[8,2]{1,0:T(8,128)} %copy.13.pairs, s32[1,2]{1,0:T(1,128)} %offsets.1, bf16[32,1024]{1,0:T(8,128)(2,1)} %bitcast.2, bf16[32,4096]{1,0:T(8,128)(2,1)} %external.1, bf16[64,96]{1,0:T(8,128)(2,1)} %constant.16.clone.refs_0_, bf16[32,192]{1,0:T(8,128)(2,1)} %constant.17.clone.refs_1_, ...), custom_call_target="tpu_custom_call" | custom-call | tf_op jit(solution)/shard_map/gradient/pallas_call | solution.py:506
  29.8 1.6 %relayout.1 = f32[32,1024]{1,0:T(8,128)} custom-call(f32[8,32,128]{2,1,0:T(8,128)} %gradient.1.slabs), custom_call_target="tpu_custom_call" | custom-call | tf_op jit(solution)/shard_map/relayout/pallas_call | solution.py:515
Async XLA Ops:
  0.0 0.7 %copy-start = (s32[8,2]{0,1:T(2,128)S(1)}, s32[8,2]{0,1:T(2,128)}, u32[]{:S(2)}) copy-start(s32[8,2]{0,1:T(2,128)} %param.14) | copy-start | bytes 196

commit v2 on v1

--- a/solution.py
+++ b/solution.py
@@ -81,6 +81,21 @@
         spread[cell, cell // side * n.grid + cell % side] = 1
     gather = np.ascontiguousarray(spread.T)
     return to_waves, from_waves, lane, lane_back, twiddle, green, spread, gather
+
+
+def far_first(n, me):
+    near = n.owners >> ((n.owners.bit_length() - 1) // 2)
+    near = n.owners // near
+    far = n.owners // near
+    z, y = me // near, lax.rem(me, near)
+    low = (z < far // 2).astype(jnp.int32)
+    here = low * (far - 1 - z) + (1 - low) * z
+    peers = []
+    for k in range(far - 1):
+        place = k + (k >= here).astype(jnp.int32)
+        level = low * (far - 1 - place) + (1 - low) * place
+        peers += [level * near + lax.rem(y + 1 + step, near) for step in range(near)]
+    return peers + [z * near + lax.rem(y + step, near) for step in range(1, near + 1)]
 
 
 def split(value):
@@ -242,18 +257,35 @@
     return dot(from_waves[...], spectrum[...])
 
 
-def kernel(n, pairs, offsets, orbital, external, *refs):
+def kernel(n, listed, placed, orbital, external, *refs):
     table_refs, refs = refs[:8], refs[8:]
     out, refs = refs[0], refs[1:]
     table_dst, refs = refs[:8], refs[8:]
     (own_box, flat, box_send, box_land, place_send, place_land, corner, near, moved, rho_send, rho_land) = refs[:11]
     (field_send, field_land, ext_block, ext_flat, dens_grid, dens_send, dens_land, level, read_in, read) = refs[11:21]
     (grad_send, stack, waves, high_ref, low_ref, back, spectrum) = refs[21:28]
-    local_sem, own_send, own_recv, grp_send, grp_recv = refs[28:]
+    pairs, listed_in, placed_in, local_sem, own_send, own_recv, grp_send, grp_recv = refs[28:]
     to_waves, from_waves, lane, lane_back, twiddle, green, spread, gather = table_dst
     owners, groups, depth, slab = n.owners, n.groups, n.depth, n.slab
     me, team = lax.axis_index("own"), lax.axis_index("grp")
-
+    partner = team + 1 - 2 * lax.rem(team, 2)
+    barrier = pltpu.get_barrier_semaphore()
+    peers = far_first(n, me)
+    for peer in peers:
+        there = {"own": peer, "grp": partner}
+        pl.semaphore_signal(barrier, inc=1, device_id=there, device_id_type=MESH)
+    base = team - lax.rem(team, 2)
+    distant = [lax.rem(base + step, groups) for step in range(2, groups)]
+    others = [*distant, partner]
+    for peer in distant:
+        pl.semaphore_signal(barrier, inc=1, device_id={"grp": peer}, device_id_type=MESH)
+
+    small_in = [
+        pltpu.make_async_copy(placed, placed_in, local_sem.at[2 + len(table_refs)]),
+        pltpu.make_async_copy(listed, listed_in, local_sem.at[3 + len(table_refs)]),
+    ]
+    for item in small_in:
+        item.start()
     own_in = pltpu.make_async_copy(orbital, own_box, local_sem.at[0])
     own_in.start()
     first_level = pl.multiple_of(me * depth // TILE * TILE, TILE)
@@ -266,16 +298,16 @@
     ]
     for item in table_in:
         item.start()
-    barrier = pltpu.get_barrier_semaphore()
-    for step in range(1, owners):
-        peer = lax.rem(me + step, owners)
-        pl.semaphore_signal(barrier, inc=1, device_id={"own": peer}, device_id_type=MESH)
-    for step in range(1, groups):
-        peer = lax.rem(team + step, groups)
-        pl.semaphore_signal(barrier, inc=1, device_id={"grp": peer}, device_id_type=MESH)
-
     row_index = lax.broadcasted_iota(jnp.int32, place_send.shape, 0)
-    place_send[...] = jnp.where(row_index == 0, offsets[0, 0], offsets[0, 1])
+    for item in small_in:
+        item.wait()
+    pair_index = lax.broadcasted_iota(jnp.int32, listed_in.shape, 1)
+    header = jnp.where(row_index == 0, placed_in[0:1, 0:1], placed_in[0:1, 1:2])
+    for turn in range(n.each):
+        mine = jnp.sum(jnp.where(pair_index == me * n.each + turn, listed_in[...], 0), axis=1, keepdims=True)
+        header = jnp.where(row_index == 2 + 2 * turn, mine[0:1], header)
+        header = jnp.where(row_index == 3 + 2 * turn, mine[1:2], header)
+    place_send[...] = header
     own_in.wait()
     for s in range(n.rows):
         flat[pl.ds(s, n.levels, stride=n.rows), :] = own_box[:, s * LANES : (s + 1) * LANES].astype(F32)
@@ -283,45 +315,53 @@
         box_send[owner] = flat[owner * slab : (owner + 1) * slab, :].astype(BF16)
     pl.semaphore_wait(barrier, owners + groups - 2)
 
-    def to_owner(phase, step, source, target):
-        peer = lax.rem(me + step, owners)
+    def to_owner(phase, peer, source, target):
         return pltpu.make_async_remote_copy(
             src_ref=source,
             dst_ref=target,
-            send_sem=own_send.at[phase, step],
-            recv_sem=own_recv.at[phase, step],
-            device_id={"own": peer},
+            send_sem=own_send.at[phase, peer],
+            recv_sem=own_recv.at[phase, me],
+            device_id={"own": peer, "grp": partner},
             device_id_type=MESH,
         )
 
-    def part(ref, index, size):
-        return ref.at[pl.ds(pl.multiple_of(index * size, size), size)]
+    def arrived(phase, source, target):
+        for peer in reversed(peers):
+            pltpu.make_async_remote_copy(
+                src_ref=source,
+                dst_ref=target(peer),
+                send_sem=own_send.at[phase, peer],
+                recv_sem=own_recv.at[phase, peer],
+                device_id={"own": peer, "grp": partner},
+                device_id_type=MESH,
+            ).wait_recv()
+
+    def rows_of(index):
+        return pl.ds(pl.multiple_of(index * slab, slab), slab)
 
     sent = []
     boxes_in = []
-    for step in range(1, owners):
-        peer = lax.rem(me + step, owners)
-        boxes_in.append(to_owner(0, step, place_send, place_land.at[me]))
-        boxes_in.append(to_owner(1, step, box_send.at[peer], box_land.at[me]))
+    for peer in peers:
+        boxes_in.append(to_owner(0, peer, place_send, place_land.at[me]))
+        boxes_in.append(to_owner(1, peer, box_send.at[peer], box_land.at[me]))
         boxes_in[-2].start()
         boxes_in[-1].start()
     sent += boxes_in
-    place_land[me] = place_send[...]
-    box_land[me] = box_send[me]
-    for item in boxes_in:
-        item.wait_recv()
+    arrived(0, place_send, lambda peer: place_land.at[peer])
+    arrived(1, box_send.at[0], lambda peer: box_land.at[peer])
     for owner in range(owners):
         corner[owner, 0] = place_land[owner, 0, 0]
         corner[owner, 1] = place_land[owner, 1, 0]
+        for turn in range(n.each):
+            pairs[owner * n.each + turn, 0] = place_land[owner, 2 + 2 * turn, 0]
+            pairs[owner * n.each + turn, 1] = place_land[owner, 3 + 2 * turn, 0]
 
     def shift_of(row):
         first, second = pairs[row, 0], pairs[row, 1]
         return corner[second, 0] - corner[first, 0], corner[second, 1] - corner[first, 1]
 
     rho_in = []
-    bundle = n.each * slab
-    for step in [*range(1, owners), 0]:
-        peer = lax.rem(me + step, owners)
+    for peer in peers:
         for turn in range(n.each):
             row = peer * n.each + turn
             dy, dx = shift_of(row)
@@ -329,15 +369,9 @@
             b = slide(n, box_land[pairs[row, 1]].astype(F32), dy, dx)
             near[row] = a
             moved[row] = b
-            if step:
-                rho_send[peer, turn] = a * b
-            else:
-                rho_land[turn, pl.ds(pl.multiple_of(me * slab, slab), slab), :] = a * b
-        if step:
-            for turn in range(n.each):
-                target = rho_land.at[turn, pl.ds(pl.multiple_of(me * slab, slab), slab)]
-                rho_in.append(to_owner(2 + turn, step, rho_send.at[peer, turn], target))
-                rho_in[-1].start()
+            rho_send[peer, turn] = a * b
+            rho_in.append(to_owner(2 + turn, peer, rho_send.at[peer, turn], rho_land.at[turn, rows_of(me)]))
+            rho_in[-1].start()
     sent += rho_in
 
     for item in table_in:
@@ -359,23 +393,23 @@
         amount = corner[owner, 0] * n.grid + corner[owner, 1]
         total = total + flat_roll(dens_grid[owner].reshape(grid_shape), amount)
     dens_send[...] = total.reshape(dens_send.shape)
-    dens_in = []
-    for step in range(1, groups):
-        dens_in.append(
-            pltpu.make_async_remote_copy(
-                src_ref=dens_send,
-                dst_ref=dens_land.at[step],
-                send_sem=grp_send.at[step],
-                recv_sem=grp_recv.at[step],
-                device_id={"grp": lax.rem(team + step, groups)},
-                device_id_type=MESH,
-            )
+    dens_land[team] = dens_send[...]
+
+    def dens_copy(peer, sender):
+        return pltpu.make_async_remote_copy(
+            src_ref=dens_send,
+            dst_ref=dens_land.at[sender],
+            send_sem=grp_send.at[peer],
+            recv_sem=grp_recv.at[sender],
+            device_id={"grp": peer},
+            device_id_type=MESH,
         )
-        dens_in[-1].start()
-    sent += dens_in
-
-    for item in rho_in:
-        item.wait_recv()
+
+    for peer in others:
+        dens_copy(peer, team).start()
+
+    for turn in range(n.each):
+        arrived(2 + turn, rho_send.at[0, turn], lambda peer: rho_land.at[turn, rows_of(peer)])
     field_in = []
     for turn in range(n.each):
         field = solve(
@@ -384,23 +418,21 @@
         )
         for s in range(n.rows):
             field_send[turn, pl.ds(s, n.levels, stride=n.rows), :] = field[:, s * LANES : (s + 1) * LANES]
-        for step in range(1, owners):
-            peer = lax.rem(me + step, owners)
-            source = field_send.at[turn, pl.ds(pl.multiple_of(peer * slab, slab), slab)]
-            field_in.append(to_owner(2 + n.each + turn, step, source, field_land.at[me * n.each + turn]))
+        for peer in peers:
+            source = field_send.at[turn, rows_of(peer)]
+            field_in.append(to_owner(2 + n.each + turn, peer, source, field_land.at[me * n.each + turn]))
             field_in[-1].start()
-        field_land[me * n.each + turn] = field_send[turn, pl.ds(pl.multiple_of(me * slab, slab), slab), :]
     sent += field_in
 
     ext_in.wait()
     ext_values = ext_block[...].astype(F32)
     for k in range(n.grid_rows):
         ext_flat[pl.ds(k, taken, stride=n.grid_rows), :] = ext_values[:, k * LANES : (k + 1) * LANES]
-    for item in dens_in:
-        item.wait_recv()
-    density = dens_send[...]
-    for step in range(1, groups):
-        density = density + dens_land[step]
+    for peer in others:
+        dens_copy(peer, peer).wait_recv()
+    density = dens_land[0]
+    for index in range(1, groups):
+        density = density + dens_land[index]
     start = pl.multiple_of((me * depth - first_level) * n.grid_rows, n.grid_rows)
     outside = ext_flat[pl.ds(start, depth * n.grid_rows), :]
     safe = jnp.where(density > 0.0, density, 1.0)
@@ -422,40 +454,31 @@
         high, low = split(value)
         read[owner] = (dot(high, gather[...]) + dot(low, gather[...])) * box_land[owner].astype(F32)
 
-    for item in field_in:
-        item.wait_recv()
+    for turn in range(n.each):
+        arrived(2 + n.each + turn, field_send.at[turn, 0:slab], lambda peer: field_land.at[peer * n.each + turn])
     for row in range(n.pairs):
         dy, dx = shift_of(row)
         field = field_land[row] * MIXING
         moved[row] = field * moved[row]
         near[row] = slide(n, field * near[row], -dy, -dx)
-    grad_in = []
-    for step in [*range(1, owners), 0]:
-        peer = lax.rem(me + step, owners)
+    for peer in peers:
         total = read[peer]
         for row in range(n.pairs):
             total = total - jnp.where(pairs[row, 0] == peer, moved[row], 0.0)
             total = total - jnp.where(pairs[row, 1] == peer, near[row], 0.0)
-        if step:
-            grad_send[peer] = total
-            grad_in.append(to_owner(2 + 2 * n.each, step, grad_send.at[peer], out.at[me]))
-            grad_in[-1].start()
-        else:
-            out[me] = total
-    sent += grad_in
-    for item in grad_in:
-        item.wait_recv()
+        grad_send[peer] = total
+        sent.append(to_owner(2 + 2 * n.each, peer, grad_send.at[peer], out.at[rows_of(me)]))
+        sent[-1].start()
+    arrived(2 + 2 * n.each, grad_send.at[0], lambda peer: out.at[rows_of(peer)])
     for item in sent:
         item.wait_send()
+    for peer in others:
+        dens_copy(peer, team).wait_send()
 
 
 def relayout_kernel(n, slabs, out):
-    for owner in range(n.owners):
-        for z in range(n.depth):
-            rows = slabs[owner, z * n.rows : (z + 1) * n.rows, :]
-            for s in range(n.rows):
-                row = owner * n.depth + z
-                out[row : row + 1, s * LANES : (s + 1) * LANES] = rows[s : s + 1, :]
+    for s in range(n.rows):
+        out[:, s * LANES : (s + 1) * LANES] = slabs[pl.ds(s, n.levels, stride=n.rows), :]
 
 
 def body(owners, groups, orbitals, offsets, pairs, ext_pot):
@@ -463,6 +486,7 @@
     n = Sizes(owners, groups, levels, cells, ext_pot.shape[1], pairs.shape[0])
     consts = tables(n)
     taken = max(n.depth, TILE)
+    header = -(-(2 + 2 * n.each) // TILE) * TILE
     slabs = (n.owners, n.slab, LANES)
     flat_rows = levels * n.rows
     scratch = [VMEM(c.shape, c.dtype) for c in consts]
@@ -471,8 +495,8 @@
         VMEM((flat_rows, LANES), F32),
         VMEM(slabs, BF16),
         VMEM(slabs, BF16),
-        VMEM((TILE, LANES), jnp.int32),
-        VMEM((owners, TILE, LANES), jnp.int32),
+        VMEM((header, LANES), jnp.int32),
+        VMEM((owners, header, LANES), jnp.int32),
         pltpu.SMEM((owners, 2), jnp.int32),
         VMEM((n.pairs, n.slab, LANES), F32),
         VMEM((n.pairs, n.slab, LANES), F32),
@@ -495,23 +519,25 @@
         VMEM((n.chunks * n.block, 2 * LANES), BF16),
         VMEM((n.chunks * n.block, 2 * LANES), F32),
         VMEM((3 * n.waves, cells), BF16),
-        pltpu.SemaphoreType.DMA((2 + len(consts),)),
+        pltpu.SMEM(pairs.shape, jnp.int32),
+        VMEM(pairs.shape[::-1], jnp.int32),
+        VMEM(offsets.shape, jnp.int32),
+        pltpu.SemaphoreType.DMA((4 + len(consts),)),
         pltpu.SemaphoreType.DMA((3 + 2 * n.each, owners)),
         pltpu.SemaphoreType.DMA((3 + 2 * n.each, owners)),
         pltpu.SemaphoreType.DMA((groups,)),
         pltpu.SemaphoreType.DMA((groups,)),
     ]
-    smem = pl.BlockSpec(memory_space=pltpu.SMEM)
     anywhere = pl.BlockSpec(memory_space=pl.ANY)
     slab_out = pl.pallas_call(
         functools.partial(kernel, n),
-        out_shape=jax.ShapeDtypeStruct(slabs, F32),
-        in_specs=[smem, smem] + [anywhere] * (2 + len(consts)),
+        out_shape=jax.ShapeDtypeStruct((flat_rows, LANES), F32),
+        in_specs=[anywhere] * (4 + len(consts)),
         out_specs=pl.BlockSpec(memory_space=VMEM),
         scratch_shapes=scratch,
         compiler_params=pltpu.CompilerParams(collective_id=0, has_side_effects=True),
         name="gradient",
-    )(pairs, offsets, orbitals[0], ext_pot, *consts)
+    )(pairs.T, offsets, orbitals[0], ext_pot, *consts)
     gradient = pl.pallas_call(
         functools.partial(relayout_kernel, n),
         out_shape=jax.ShapeDtypeStruct((levels, cells), F32),

time: 31.6 us -> 28.9 us (0.915)
  the two profiles are of different devices: /device:TPU:0 before, /device:TPU:1 now
where the time goes in v2:
time: 28.9 us; the launch traced here: 28.8 us
  Pallas kernels  28.7 us (99%)
    pallas_call x1, Pallas kernels, body(): pl.pallas_call(functools.partial(kernel, n), out_shape=jax.ShapeDtypeStru...  27.2 us
    pallas_call x1, Pallas kernels, body(): pl.pallas_call(functools.partial(relayout_kernel, n), out_shape=jax.Shape...  1.58 us

profile of v2, /device:TPU:1, one launch (start us, length us, event | category | flops | bytes accessed | tf_op | source)
XLA Modules:
  0.0 28.8 jit_solution(16422202500668858053)
XLA Ops:
  0.0 27.2 %gradient.1.slabs = f32[256,128]{1,0:T(8,128)} custom-call(s32[2,8]{1,0:T(2,128)} %bitcast.4, s32[1,2]{1,0:T(1,128)} %placed.1, bf16[32,1024]{1,0:T(8,128)(2,1)} %bitcast.3, bf16[32,4096]{1,0:T(8,128)(2,1)} %external.1, bf16[64,96]{1,0:T(8,128)(2,1)} %constant.16.clone.refs_0_, bf16[32,192]{1,0:T(8,128)(2,1)} %constant.17.clone.refs_1_, ...), custom_call_target="tpu_custom_call" | custom-call | tf_op jit(solution)/shard_map/gradient/pallas_call | solution.py:532
  27.2 1.6 %relayout.1 = f32[32,1024]{1,0:T(8,128)} custom-call(f32[256,128]{1,0:T(8,128)} %gradient.1.slabs), custom_call_target="tpu_custom_call" | custom-call | tf_op jit(solution)/shard_map/relayout/pallas_call | solution.py:541

commit v3 on v2

--- a/solution.py
+++ b/solution.py
@@ -15,7 +15,6 @@
 EXCHANGE_COEF = (3.0 / math.pi) ** (1.0 / 3.0)
 LANES = 128
 TILE = 8
-CHUNK = 16
 VMEM = pltpu.VMEM
 MESH = pl.DeviceIdType.MESH
 F32 = jnp.float32
@@ -36,8 +35,8 @@
         self.waves = 2 * levels
         self.turns = 2 * self.side // self.per
         self.wide = self.per * 2 * self.side
-        self.block = self.turns * CHUNK
-        self.chunks = self.waves // CHUNK
+        self.bands = levels // TILE
+        self.share = TILE // self.depth
 
 
 def halves_of(table):
@@ -71,11 +70,11 @@
         m = np.arange(length)
         return (2.0 * np.pi / length * np.where(m < length // 2, m, m - length)) ** 2
 
-    z = squares(n.waves).reshape(n.chunks, 1, CHUNK, 1, 1)
-    y = squares(2 * side).reshape(per, n.turns).T.reshape(1, n.turns, 1, per, 1)
-    x = squares(2 * side).reshape(1, 1, 1, 1, 2 * side)
+    z = squares(n.waves).reshape(n.waves, 1, 1, 1)
+    y = squares(2 * side).reshape(per, n.turns).T.reshape(1, n.turns, per, 1)
+    x = squares(2 * side).reshape(1, 1, 1, 2 * side)
     green = 4.0 * np.pi / (z + y + x + SCREEN) / (n.waves * 4.0 * side * side)
-    green = green.reshape(n.chunks * n.block, n.wide).astype(np.float32)
+    green = green.reshape(n.waves, n.turns * n.wide).astype(np.float32)
     spread = np.zeros((LANES, n.halves * LANES), ml_dtypes.bfloat16)
     for cell in range(LANES):
         spread[cell, cell // side * n.grid + cell % side] = 1
@@ -198,63 +197,65 @@
     return values
 
 
-def solve(n, rho, stack, waves, high_ref, low_ref, back, spectrum, to_waves, from_waves, lane, lane_back, twiddle, green):
-    levels = n.levels
-    for s in range(n.rows):
-        columns = slice(s * LANES, (s + 1) * LANES)
-        high, low = split(rho[pl.ds(s, levels, stride=n.rows), :])
-        stack[0:levels, columns] = high
-        stack[levels : 2 * levels, columns] = low
-        stack[2 * levels : 3 * levels, columns] = high
-    waves[...] = dot(to_waves[...], stack[...])
+def forward_band(n, rho, band, planes, lane, twiddle):
+    start = pl.multiple_of(band * (TILE * n.rows), TILE * n.rows)
+    values = [rho[pl.ds(start + s, TILE, stride=n.rows), :] for s in range(n.rows)]
+    cosines, sines = wave_sums(n, values)
     top = n.turns // 2
-    for chunk in range(n.chunks):
-        band = slice(chunk * CHUNK, (chunk + 1) * CHUNK)
-        cosines, sines = wave_sums(n, [waves[band, s * LANES : (s + 1) * LANES] for s in range(n.rows)])
-        for q in range(n.turns):
-            same = q <= top
-            a = cosines[q if same else n.turns - q]
-            b = sines[q if same else n.turns - q]
-            ahead = twiddle[q : q + 1, :]
-            behind = twiddle[n.turns + q : n.turns + q + 1, :]
-            u, w = ahead * a, behind * a
-            if b is not None and q % top:
-                u = u + behind * b if same else u - behind * b
-                w = w - ahead * b if same else w + ahead * b
-            rows = slice(chunk * n.block + q * CHUNK, chunk * n.block + (q + 1) * CHUNK)
-            for index, part in enumerate((u, w)):
-                columns = slice(index * LANES, (index + 1) * LANES)
-                high_ref[rows, columns], low_ref[rows, columns] = split(part)
-    for chunk in range(n.chunks):
-        rows = slice(chunk * n.block, (chunk + 1) * n.block)
-        value = thrice(high_ref[rows, :], low_ref[rows, :], lane) * green[rows, :]
-        high, low = split(value)
-        back[rows, :] = thrice(high, low, lane_back)
-    for chunk in range(n.chunks):
-        cosines, sines = [None] * (top + 1), [None] * (top + 1)
-        for q in range(n.turns):
-            rows = slice(chunk * n.block + q * CHUNK, chunk * n.block + (q + 1) * CHUNK)
-            u, w = back[rows, 0:LANES], back[rows, LANES : 2 * LANES]
-            ahead = twiddle[q : q + 1, :]
-            behind = twiddle[n.turns + q : n.turns + q + 1, :]
-            a = ahead * u + behind * w
-            if q <= top:
-                cosines[q] = a
-            else:
-                cosines[n.turns - q] = cosines[n.turns - q] + a
-            if q % top:
-                b = behind * u - ahead * w
-                sines[q if q <= top else n.turns - q] = (
-                    b if q <= top else sines[n.turns - q] - b
-                )
-        values = cell_sums(n, cosines, sines)
-        for s in range(n.rows):
-            columns = slice(s * LANES, (s + 1) * LANES)
-            high, low = split(values[s])
-            for place, part in enumerate((high, low, high)):
-                start = place * n.waves + chunk * CHUNK
-                spectrum[start : start + CHUNK, columns] = part
-    return dot(from_waves[...], spectrum[...])
+    first, second = [], []
+    for q in range(n.turns):
+        same = q <= top
+        a = cosines[q if same else n.turns - q]
+        b = sines[q if same else n.turns - q]
+        ahead = twiddle[q : q + 1, :]
+        behind = twiddle[n.turns + q : n.turns + q + 1, :]
+        u, w = ahead * a, behind * a
+        if q % top:
+            u = u + behind * b if same else u - behind * b
+            w = w - ahead * b if same else w + ahead * b
+        first.append(u)
+        second.append(w)
+    value = jnp.concatenate([jnp.concatenate(first, axis=0), jnp.concatenate(second, axis=0)], axis=1)
+    high, low = split(value)
+    value = thrice(high, low, lane)
+    rows = pl.ds(pl.multiple_of(band * TILE, TILE), TILE)
+    for q in range(n.turns):
+        planes[rows, q * n.wide : (q + 1) * n.wide] = value[q * TILE : (q + 1) * TILE, :]
+
+
+def stacked(value):
+    high, low = split(value)
+    return jnp.concatenate([high, low, high], axis=0)
+
+
+def along_z(planes, to_waves, from_waves, green):
+    value = dot(to_waves[...], stacked(planes[...])) * green[...]
+    planes[...] = dot(from_waves[...], stacked(value))
+
+
+def back_band(n, planes, band, field, lane_back, twiddle):
+    rows = pl.ds(pl.multiple_of(band * TILE, TILE), TILE)
+    value = jnp.concatenate([planes[rows, q * n.wide : (q + 1) * n.wide] for q in range(n.turns)], axis=0)
+    high, low = split(value)
+    value = thrice(high, low, lane_back)
+    top = n.turns // 2
+    cosines, sines = [None] * (top + 1), [None] * (top + 1)
+    for q in range(n.turns):
+        part = slice(q * TILE, (q + 1) * TILE)
+        u, w = value[part, 0:LANES], value[part, LANES : 2 * LANES]
+        ahead = twiddle[q : q + 1, :]
+        behind = twiddle[n.turns + q : n.turns + q + 1, :]
+        a = ahead * u + behind * w
+        b = behind * u - ahead * w
+        if q <= top:
+            cosines[q] = a
+            sines[q] = b if q % top else None
+        else:
+            cosines[n.turns - q] = cosines[n.turns - q] + a
+            sines[n.turns - q] = sines[n.turns - q] - b
+    start = pl.multiple_of(band * (TILE * n.rows), TILE * n.rows)
+    for s, part in enumerate(cell_sums(n, cosines, sines)):
+        field[pl.ds(start + s, TILE, stride=n.rows), :] = part
 
 
 def kernel(n, listed, placed, orbital, external, *refs):
@@ -263,8 +264,8 @@
     table_dst, refs = refs[:8], refs[8:]
     (own_box, flat, box_send, box_land, place_send, place_land, corner, near, moved, rho_send, rho_land) = refs[:11]
     (field_send, field_land, ext_block, ext_flat, dens_grid, dens_send, dens_land, level, read_in, read) = refs[11:21]
-    (grad_send, stack, waves, high_ref, low_ref, back, spectrum) = refs[21:28]
-    pairs, listed_in, placed_in, local_sem, own_send, own_recv, grp_send, grp_recv = refs[28:]
+    (grad_send, planes, pairs, listed_in, placed_in) = refs[21:26]
+    local_sem, own_send, own_recv, grp_send, grp_recv = refs[26:]
     to_waves, from_waves, lane, lane_back, twiddle, green, spread, gather = table_dst
     owners, groups, depth, slab = n.owners, n.groups, n.depth, n.slab
     me, team = lax.axis_index("own"), lax.axis_index("grp")
@@ -325,16 +326,19 @@
             device_id_type=MESH,
         )
 
+    def arrive(phase, peer, source, target):
+        pltpu.make_async_remote_copy(
+            src_ref=source,
+            dst_ref=target,
+            send_sem=own_send.at[phase, peer],
+            recv_sem=own_recv.at[phase, peer],
+            device_id={"own": peer, "grp": partner},
+            device_id_type=MESH,
+        ).wait_recv()
+
     def arrived(phase, source, target):
         for peer in reversed(peers):
-            pltpu.make_async_remote_copy(
-                src_ref=source,
-                dst_ref=target(peer),
-                send_sem=own_send.at[phase, peer],
-                recv_sem=own_recv.at[phase, peer],
-                device_id={"own": peer, "grp": partner},
-                device_id_type=MESH,
-            ).wait_recv()
+            arrive(phase, peer, source, target(peer))
 
     def rows_of(index):
         return pl.ds(pl.multiple_of(index * slab, slab), slab)
@@ -408,20 +412,23 @@
     for peer in others:
         dens_copy(peer, team).start()
 
-    for turn in range(n.each):
-        arrived(2 + turn, rho_send.at[0, turn], lambda peer: rho_land.at[turn, rows_of(peer)])
+    low = (me < owners // 2).astype(jnp.int32)
+    far_bands = [low * (n.bands - 1 - k) + (1 - low) * k for k in range(n.bands)]
     field_in = []
     for turn in range(n.each):
-        field = solve(
-            n, rho_land.at[turn], stack, waves, high_ref, low_ref, back, spectrum,
-            to_waves, from_waves, lane, lane_back, twiddle, green,
-        )
-        for s in range(n.rows):
-            field_send[turn, pl.ds(s, n.levels, stride=n.rows), :] = field[:, s * LANES : (s + 1) * LANES]
-        for peer in peers:
-            source = field_send.at[turn, rows_of(peer)]
-            field_in.append(to_owner(2 + n.each + turn, peer, source, field_land.at[me * n.each + turn]))
-            field_in[-1].start()
+        for band in reversed(far_bands):
+            for index in range(n.share):
+                peer = band * n.share + index
+                arrive(2 + turn, peer, rho_send.at[0, turn], rho_land.at[turn, rows_of(peer)])
+            forward_band(n, rho_land.at[turn], band, planes, lane, twiddle)
+        along_z(planes, to_waves, from_waves, green)
+        for band in far_bands:
+            back_band(n, planes, band, field_send.at[turn], lane_back, twiddle)
+            for index in range(n.share):
+                peer = band * n.share + index
+                source = field_send.at[turn, rows_of(peer)]
+                field_in.append(to_owner(2 + n.each + turn, peer, source, field_land.at[me * n.each + turn]))
+                field_in[-1].start()
     sent += field_in
 
     ext_in.wait()
@@ -474,11 +481,6 @@
         item.wait_send()
     for peer in others:
         dens_copy(peer, team).wait_send()
-
-
-def relayout_kernel(n, slabs, out):
-    for s in range(n.rows):
-        out[:, s * LANES : (s + 1) * LANES] = slabs[pl.ds(s, n.levels, stride=n.rows), :]
 
 
 def body(owners, groups, orbitals, offsets, pairs, ext_pot):
@@ -513,12 +515,7 @@
         VMEM((owners, n.depth * n.grid_rows, LANES), F32),
         VMEM(slabs, F32),
         VMEM(slabs, F32),
-        VMEM((3 * levels, cells), BF16),
-        VMEM((n.waves, cells), F32),
-        VMEM((n.chunks * n.block, 2 * LANES), BF16),
-        VMEM((n.chunks * n.block, 2 * LANES), BF16),
-        VMEM((n.chunks * n.block, 2 * LANES), F32),
-        VMEM((3 * n.waves, cells), BF16),
+        VMEM((levels, n.turns * n.wide), F32),
         pltpu.SMEM(pairs.shape, jnp.int32),
         VMEM(pairs.shape[::-1], jnp.int32),
         VMEM(offsets.shape, jnp.int32),
@@ -531,21 +528,14 @@
     anywhere = pl.BlockSpec(memory_space=pl.ANY)
     slab_out = pl.pallas_call(
         functools.partial(kernel, n),
-        out_shape=jax.ShapeDtypeStruct((flat_rows, LANES), F32),
+        out_shape=VMEM((flat_rows, LANES), F32),
         in_specs=[anywhere] * (4 + len(consts)),
         out_specs=pl.BlockSpec(memory_space=VMEM),
         scratch_shapes=scratch,
         compiler_params=pltpu.CompilerParams(collective_id=0, has_side_effects=True),
         name="gradient",
     )(pairs.T, offsets, orbitals[0], ext_pot, *consts)
-    gradient = pl.pallas_call(
-        functools.partial(relayout_kernel, n),
-        out_shape=jax.ShapeDtypeStruct((levels, cells), F32),
-        in_specs=[pl.BlockSpec(memory_space=VMEM)],
-        out_specs=pl.BlockSpec(memory_space=VMEM),
-        name="relayout",
-    )(slab_out)
-    return gradient[None]
+    return slab_out.reshape(1, levels, cells)
 
 
 def solution(mesh):

time: 28.9 us -> 27.2 us (0.941)
  Pallas kernels: 28.7 us -> 26.4 us
  local copies, waits for them, and re-layouts: 0 us -> 0.68 us
    pallas_call x2 -> x1, Pallas kernels: 28.7 us -> 26.4 us  [body(): pl.pallas_call(functools.partial(kernel, n), out_shape=VMEM((flat_rows, L...]
    reshape x0 -> x1, local copies, waits for them, and re-layouts: none -> 0.68 us  [body(): return slab_out.reshape(1, levels, cells)]
where the time goes in v3:
time: 27.2 us; the launch traced here: 27.1 us
  Pallas kernels  26.4 us (97%)
  local copies, waits for them, and re-layouts  0.68 us (2%)
    pallas_call x1, Pallas kernels, body(): pl.pallas_call(functools.partial(kernel, n), out_shape=VMEM((flat_rows, L...  26.4 us
    reshape x1, local copies, waits for them, and re-layouts, body(): return slab_out.reshape(1, levels, cells)  0.68 us

profile of v3, /device:TPU:1, one launch (start us, length us, event | category | flops | bytes accessed | tf_op | source)
XLA Modules:
  0.0 27.1 jit_solution(13613153368089169157)
XLA Ops:
  0.0 26.4 %gradient.1 = f32[256,128]{1,0:T(8,128)S(1)} custom-call(s32[2,8]{1,0:T(2,128)} %bitcast.3, s32[1,2]{1,0:T(1,128)} %placed.1, bf16[32,1024]{1,0:T(8,128)(2,1)} %bitcast.2, bf16[32,4096]{1,0:T(8,128)(2,1)} %external.1, bf16[64,96]{1,0:T(8,128)(2,1)} %constant.16.clone.refs_0_, bf16[32,192]{1,0:T(8,128)(2,1)} %constant.17.clone.refs_1_, ...), custom_call_target="tpu_custom_call" | custom-call | tf_op jit(solution)/shard_map/gradient/pallas_call | solution.py:529
  26.4 0.7 %reshape.3 = f32[1,32,1024]{2,1,0:T(8,128)} reshape(f32[256,128]{1,0:T(8,128)S(1)} %gradient.1) | data formatting | bytes 262144 | tf_op jit(solution)/shard_map/reshape | solution.py:538

commit v4 on v3

--- a/solution.py
+++ b/solution.py
@@ -299,15 +299,15 @@
     ]
     for item in table_in:
         item.start()
-    row_index = lax.broadcasted_iota(jnp.int32, place_send.shape, 0)
+    place_index = lax.broadcasted_iota(jnp.int32, place_send.shape, 1)
     for item in small_in:
         item.wait()
     pair_index = lax.broadcasted_iota(jnp.int32, listed_in.shape, 1)
-    header = jnp.where(row_index == 0, placed_in[0:1, 0:1], placed_in[0:1, 1:2])
+    header = jnp.where(place_index == 0, placed_in[0:1, 0:1], placed_in[0:1, 1:2])
     for turn in range(n.each):
         mine = jnp.sum(jnp.where(pair_index == me * n.each + turn, listed_in[...], 0), axis=1, keepdims=True)
-        header = jnp.where(row_index == 2 + 2 * turn, mine[0:1], header)
-        header = jnp.where(row_index == 3 + 2 * turn, mine[1:2], header)
+        header = jnp.where(place_index == 2 + 2 * turn, mine[0:1], header)
+        header = jnp.where(place_index == 3 + 2 * turn, mine[1:2], header)
     place_send[...] = header
     own_in.wait()
     for s in range(n.rows):
@@ -355,10 +355,10 @@
     arrived(1, box_send.at[0], lambda peer: box_land.at[peer])
     for owner in range(owners):
         corner[owner, 0] = place_land[owner, 0, 0]
-        corner[owner, 1] = place_land[owner, 1, 0]
+        corner[owner, 1] = place_land[owner, 0, 1]
         for turn in range(n.each):
-            pairs[owner * n.each + turn, 0] = place_land[owner, 2 + 2 * turn, 0]
-            pairs[owner * n.each + turn, 1] = place_land[owner, 3 + 2 * turn, 0]
+            pairs[owner * n.each + turn, 0] = place_land[owner, 0, 2 + 2 * turn]
+            pairs[owner * n.each + turn, 1] = place_land[owner, 0, 3 + 2 * turn]
 
     def shift_of(row):
         first, second = pairs[row, 0], pairs[row, 1]
@@ -488,7 +488,6 @@
     n = Sizes(owners, groups, levels, cells, ext_pot.shape[1], pairs.shape[0])
     consts = tables(n)
     taken = max(n.depth, TILE)
-    header = -(-(2 + 2 * n.each) // TILE) * TILE
     slabs = (n.owners, n.slab, LANES)
     flat_rows = levels * n.rows
     scratch = [VMEM(c.shape, c.dtype) for c in consts]
@@ -497,8 +496,8 @@
         VMEM((flat_rows, LANES), F32),
         VMEM(slabs, BF16),
         VMEM(slabs, BF16),
-        VMEM((header, LANES), jnp.int32),
-        VMEM((owners, header, LANES), jnp.int32),
+        VMEM((1, LANES), jnp.int32),
+        VMEM((owners, 1, LANES), jnp.int32),
         pltpu.SMEM((owners, 2), jnp.int32),
         VMEM((n.pairs, n.slab, LANES), F32),
         VMEM((n.pairs, n.slab, LANES), F32),

time: 27.2 us -> 26.2 us (0.963)
  the two profiles are of different devices: /device:TPU:1 before, /device:TPU:0 now
where the time goes in v4:
time: 26.2 us; the launch traced here: 25.9 us
  Pallas kernels  25.2 us (96%)
  local copies, waits for them, and re-layouts  0.68 us (3%)
    pallas_call x1, Pallas kernels, body(): pl.pallas_call(functools.partial(kernel, n), out_shape=VMEM((flat_rows, L...  25.2 us
    reshape x1, local copies, waits for them, and re-layouts, body(): return slab_out.reshape(1, levels, cells)  0.68 us

profile of v4, /device:TPU:0, one launch (start us, length us, event | category | flops | bytes accessed | tf_op | source)
XLA Modules:
  0.0 25.9 jit_solution(11105986606646674682)
XLA Ops:
  0.0 25.2 %gradient.1 = f32[256,128]{1,0:T(8,128)S(1)} custom-call(s32[2,8]{1,0:T(2,128)} %bitcast.3, s32[1,2]{1,0:T(1,128)} %placed.1, bf16[32,1024]{1,0:T(8,128)(2,1)} %bitcast.2, bf16[32,4096]{1,0:T(8,128)(2,1)} %external.1, bf16[64,96]{1,0:T(8,128)(2,1)} %constant.16.clone.refs_0_, bf16[32,192]{1,0:T(8,128)(2,1)} %constant.17.clone.refs_1_, ...), custom_call_target="tpu_custom_call" | custom-call | tf_op jit(solution)/shard_map/gradient/pallas_call | solution.py:528
  25.2 0.7 %reshape.3 = f32[1,32,1024]{2,1,0:T(8,128)} reshape(f32[256,128]{1,0:T(8,128)S(1)} %gradient.1) | data formatting | bytes 262144 | tf_op jit(solution)/shard_map/reshape | solution.py:537

commit v5 on v4

--- a/solution.py
+++ b/solution.py
@@ -19,6 +19,9 @@
 MESH = pl.DeviceIdType.MESH
 F32 = jnp.float32
 BF16 = jnp.bfloat16
+CODE = jnp.int16
+STEPS = 32767.0
+TINY = 1e-30
 
 
 class Sizes:
@@ -100,6 +103,17 @@
 def split(value):
     high = value.astype(BF16)
     return high, (value - high.astype(F32)).astype(BF16)
+
+
+def encode(value):
+    largest = jnp.max(jnp.abs(value), axis=0, keepdims=True)
+    largest = jnp.maximum(largest, TINY)
+    code = jnp.round(value * (STEPS / largest)).astype(jnp.int32)
+    return code.astype(CODE), largest * (1.0 / STEPS)
+
+
+def decode(code, step):
+    return code.astype(jnp.int32).astype(F32) * step
 
 
 def dot(left, right):
@@ -262,10 +276,11 @@
     table_refs, refs = refs[:8], refs[8:]
     out, refs = refs[0], refs[1:]
     table_dst, refs = refs[:8], refs[8:]
-    (own_box, flat, box_send, box_land, place_send, place_land, corner, near, moved, rho_send, rho_land) = refs[:11]
-    (field_send, field_land, ext_block, ext_flat, dens_grid, dens_send, dens_land, level, read_in, read) = refs[11:21]
-    (grad_send, planes, pairs, listed_in, placed_in) = refs[21:26]
-    local_sem, own_send, own_recv, grp_send, grp_recv = refs[26:]
+    (own_box, flat, box_send, box_land, place_send, place_land, corner, near, moved, rho, field_flat) = refs[:11]
+    (ext_block, ext_flat, dens_grid, dens_send, dens_land, level, read_in, read, planes, pairs) = refs[11:21]
+    (listed_in, placed_in, rho_send, rho_land, field_send, field_land, grad_send, grad_land) = refs[21:29]
+    (rho_step, rho_steps, field_step, field_steps, grad_step, grad_steps) = refs[29:35]
+    local_sem, own_send, own_recv, grp_send, grp_recv = refs[35:]
     to_waves, from_waves, lane, lane_back, twiddle, green, spread, gather = table_dst
     owners, groups, depth, slab = n.owners, n.groups, n.depth, n.slab
     me, team = lax.axis_index("own"), lax.axis_index("grp")
@@ -343,6 +358,23 @@
     def rows_of(index):
         return pl.ds(pl.multiple_of(index * slab, slab), slab)
 
+    def send_coded(phase, peer, value, here, there):
+        slot, codes, steps = here
+        codes[slot], steps[slot] = encode(value)
+        landing, far_codes, far_steps = there
+        copies = [
+            to_owner(phase, peer, codes.at[slot], far_codes.at[landing]),
+            to_owner(phase + 1, peer, steps.at[slot], far_steps.at[landing]),
+        ]
+        for item in copies:
+            item.start()
+        return copies
+
+    def take_coded(phase, peer, slot, codes, steps):
+        arrive(phase, peer, codes.at[slot], codes.at[slot])
+        arrive(phase + 1, peer, steps.at[slot], steps.at[slot])
+        return decode(codes[slot], steps[slot])
+
     sent = []
     boxes_in = []
     for peer in peers:
@@ -373,9 +405,7 @@
             b = slide(n, box_land[pairs[row, 1]].astype(F32), dy, dx)
             near[row] = a
             moved[row] = b
-            rho_send[peer, turn] = a * b
-            rho_in.append(to_owner(2 + turn, peer, rho_send.at[peer, turn], rho_land.at[turn, rows_of(me)]))
-            rho_in[-1].start()
+            rho_in += send_coded(2 + 2 * turn, peer, a * b, (row, rho_send, rho_step), (me * n.each + turn, rho_land, rho_steps))
     sent += rho_in
 
     for item in table_in:
@@ -414,21 +444,24 @@
 
     low = (me < owners // 2).astype(jnp.int32)
     far_bands = [low * (n.bands - 1 - k) + (1 - low) * k for k in range(n.bands)]
+    rho_base = 2
+    field_base = rho_base + 2 * n.each
+    grad_base = field_base + 2 * n.each
     field_in = []
     for turn in range(n.each):
         for band in reversed(far_bands):
             for index in range(n.share):
                 peer = band * n.share + index
-                arrive(2 + turn, peer, rho_send.at[0, turn], rho_land.at[turn, rows_of(peer)])
-            forward_band(n, rho_land.at[turn], band, planes, lane, twiddle)
+                rho[rows_of(peer), :] = take_coded(rho_base + 2 * turn, peer, peer * n.each + turn, rho_land, rho_steps)
+            forward_band(n, rho, band, planes, lane, twiddle)
         along_z(planes, to_waves, from_waves, green)
         for band in far_bands:
-            back_band(n, planes, band, field_send.at[turn], lane_back, twiddle)
+            back_band(n, planes, band, field_flat, lane_back, twiddle)
             for index in range(n.share):
                 peer = band * n.share + index
-                source = field_send.at[turn, rows_of(peer)]
-                field_in.append(to_owner(2 + n.each + turn, peer, source, field_land.at[me * n.each + turn]))
-                field_in[-1].start()
+                slot = peer * n.each + turn
+                here, there = (slot, field_send, field_step), (me * n.each + turn, field_land, field_steps)
+                field_in += send_coded(field_base + 2 * turn, peer, field_flat[rows_of(peer), :], here, there)
     sent += field_in
 
     ext_in.wait()
@@ -461,22 +494,21 @@
         high, low = split(value)
         read[owner] = (dot(high, gather[...]) + dot(low, gather[...])) * box_land[owner].astype(F32)
 
-    for turn in range(n.each):
-        arrived(2 + n.each + turn, field_send.at[turn, 0:slab], lambda peer: field_land.at[peer * n.each + turn])
-    for row in range(n.pairs):
-        dy, dx = shift_of(row)
-        field = field_land[row] * MIXING
-        moved[row] = field * moved[row]
-        near[row] = slide(n, field * near[row], -dy, -dx)
+    for peer in reversed(peers):
+        for turn in range(n.each):
+            row = peer * n.each + turn
+            dy, dx = shift_of(row)
+            field = take_coded(field_base + 2 * turn, peer, row, field_land, field_steps) * MIXING
+            moved[row] = field * moved[row]
+            near[row] = slide(n, field * near[row], -dy, -dx)
     for peer in peers:
         total = read[peer]
         for row in range(n.pairs):
             total = total - jnp.where(pairs[row, 0] == peer, moved[row], 0.0)
             total = total - jnp.where(pairs[row, 1] == peer, near[row], 0.0)
-        grad_send[peer] = total
-        sent.append(to_owner(2 + 2 * n.each, peer, grad_send.at[peer], out.at[rows_of(me)]))
-        sent[-1].start()
-    arrived(2 + 2 * n.each, grad_send.at[0], lambda peer: out.at[rows_of(peer)])
+        sent += send_coded(grad_base, peer, total, (peer, grad_send, grad_step), (me, grad_land, grad_steps))
+    for peer in reversed(peers):
+        out[rows_of(peer), :] = take_coded(grad_base, peer, peer, grad_land, grad_steps)
     for item in sent:
         item.wait_send()
     for peer in others:
@@ -491,6 +523,7 @@
     slabs = (n.owners, n.slab, LANES)
     flat_rows = levels * n.rows
     scratch = [VMEM(c.shape, c.dtype) for c in consts]
+    counts = (n.pairs, n.pairs, n.pairs, n.pairs, owners, owners)
     scratch += [
         VMEM((levels, cells), BF16),
         VMEM((flat_rows, LANES), F32),
@@ -501,10 +534,8 @@
         pltpu.SMEM((owners, 2), jnp.int32),
         VMEM((n.pairs, n.slab, LANES), F32),
         VMEM((n.pairs, n.slab, LANES), F32),
-        VMEM((owners, n.each, n.slab, LANES), F32),
-        VMEM((n.each, flat_rows, LANES), F32),
-        VMEM((n.each, flat_rows, LANES), F32),
-        VMEM((n.pairs, n.slab, LANES), F32),
+        VMEM((flat_rows, LANES), F32),
+        VMEM((flat_rows, LANES), F32),
         VMEM((taken, ext_pot.shape[1]), BF16),
         VMEM((taken * n.grid_rows, LANES), F32),
         VMEM((owners, n.depth * n.grid_rows, LANES), F32),
@@ -513,14 +544,15 @@
         VMEM((n.depth * n.grid_rows, LANES), F32),
         VMEM((owners, n.depth * n.grid_rows, LANES), F32),
         VMEM(slabs, F32),
-        VMEM(slabs, F32),
         VMEM((levels, n.turns * n.wide), F32),
         pltpu.SMEM(pairs.shape, jnp.int32),
         VMEM(pairs.shape[::-1], jnp.int32),
         VMEM(offsets.shape, jnp.int32),
+        *[VMEM((count, n.slab, LANES), CODE) for count in counts],
+        *[VMEM((count, 1, LANES), F32) for count in counts],
         pltpu.SemaphoreType.DMA((4 + len(consts),)),
-        pltpu.SemaphoreType.DMA((3 + 2 * n.each, owners)),
-        pltpu.SemaphoreType.DMA((3 + 2 * n.each, owners)),
+        pltpu.SemaphoreType.DMA((4 + 4 * n.each, owners)),
+        pltpu.SemaphoreType.DMA((4 + 4 * n.each, owners)),
         pltpu.SemaphoreType.DMA((groups,)),
         pltpu.SemaphoreType.DMA((groups,)),
     ]

time: 26.2 us -> 25.2 us (0.962)
  Pallas kernels: 25.2 us -> 24.3 us
    pallas_call x1, Pallas kernels: 25.2 us -> 24.3 us  [body(): pl.pallas_call(functools.partial(kernel, n), out_shape=VMEM((flat_rows, L...]
where the time goes in v5:
time: 25.2 us; the launch traced here: 25 us
  Pallas kernels  24.3 us (96%)
  local copies, waits for them, and re-layouts  0.68 us (3%)
    pallas_call x1, Pallas kernels, body(): pl.pallas_call(functools.partial(kernel, n), out_shape=VMEM((flat_rows, L...  24.3 us
    reshape x1, local copies, waits for them, and re-layouts, body(): return slab_out.reshape(1, levels, cells)  0.68 us

profile of v5, /device:TPU:0, one launch (start us, length us, event | category | flops | bytes accessed | tf_op | source)
XLA Modules:
  0.0 25.0 jit_solution(17147818870838235336)
XLA Ops:
  0.0 24.3 %gradient.1 = f32[256,128]{1,0:T(8,128)S(1)} custom-call(s32[2,8]{1,0:T(2,128)} %bitcast.3, s32[1,2]{1,0:T(1,128)} %placed.1, bf16[32,1024]{1,0:T(8,128)(2,1)} %bitcast.2, bf16[32,4096]{1,0:T(8,128)(2,1)} %external.1, bf16[64,96]{1,0:T(8,128)(2,1)} %constant.16.clone.refs_0_, bf16[32,192]{1,0:T(8,128)(2,1)} %constant.17.clone.refs_1_, ...), custom_call_target="tpu_custom_call" | custom-call | tf_op jit(solution)/shard_map/gradient/pallas_call | solution.py:560
  24.4 0.7 %reshape.3 = f32[1,32,1024]{2,1,0:T(8,128)} reshape(f32[256,128]{1,0:T(8,128)S(1)} %gradient.1) | data formatting | bytes 262144 | tf_op jit(solution)/shard_map/reshape | solution.py:569

commit v6 on v5

--- a/solution.py
+++ b/solution.py
@@ -15,6 +15,8 @@
 EXCHANGE_COEF = (3.0 / math.pi) ** (1.0 / 3.0)
 LANES = 128
 TILE = 8
+AHEAD = 16
+BEHIND = 8
 VMEM = pltpu.VMEM
 MESH = pl.DeviceIdType.MESH
 F32 = jnp.float32
@@ -38,8 +40,7 @@
         self.waves = 2 * levels
         self.turns = 2 * self.side // self.per
         self.wide = self.per * 2 * self.side
-        self.bands = levels // TILE
-        self.share = TILE // self.depth
+        self.ahead, self.behind = min(AHEAD, levels), min(BEHIND, levels)
 
 
 def halves_of(table):
@@ -211,9 +212,9 @@
     return values
 
 
-def forward_band(n, rho, band, planes, lane, twiddle):
-    start = pl.multiple_of(band * (TILE * n.rows), TILE * n.rows)
-    values = [rho[pl.ds(start + s, TILE, stride=n.rows), :] for s in range(n.rows)]
+def forward_band(n, rho, band, size, planes, lane, twiddle):
+    start = pl.multiple_of(band * (size * n.rows), size * n.rows)
+    values = [rho[pl.ds(start + s, size, stride=n.rows), :] for s in range(n.rows)]
     cosines, sines = wave_sums(n, values)
     top = n.turns // 2
     first, second = [], []
@@ -232,9 +233,9 @@
     value = jnp.concatenate([jnp.concatenate(first, axis=0), jnp.concatenate(second, axis=0)], axis=1)
     high, low = split(value)
     value = thrice(high, low, lane)
-    rows = pl.ds(pl.multiple_of(band * TILE, TILE), TILE)
+    rows = pl.ds(pl.multiple_of(band * size, size), size)
     for q in range(n.turns):
-        planes[rows, q * n.wide : (q + 1) * n.wide] = value[q * TILE : (q + 1) * TILE, :]
+        planes[rows, q * n.wide : (q + 1) * n.wide] = value[q * size : (q + 1) * size, :]
 
 
 def stacked(value):
@@ -247,15 +248,15 @@
     planes[...] = dot(from_waves[...], stacked(value))
 
 
-def back_band(n, planes, band, field, lane_back, twiddle):
-    rows = pl.ds(pl.multiple_of(band * TILE, TILE), TILE)
+def back_band(n, planes, band, size, field, lane_back, twiddle):
+    rows = pl.ds(pl.multiple_of(band * size, size), size)
     value = jnp.concatenate([planes[rows, q * n.wide : (q + 1) * n.wide] for q in range(n.turns)], axis=0)
     high, low = split(value)
     value = thrice(high, low, lane_back)
     top = n.turns // 2
     cosines, sines = [None] * (top + 1), [None] * (top + 1)
     for q in range(n.turns):
-        part = slice(q * TILE, (q + 1) * TILE)
+        part = slice(q * size, (q + 1) * size)
         u, w = value[part, 0:LANES], value[part, LANES : 2 * LANES]
         ahead = twiddle[q : q + 1, :]
         behind = twiddle[n.turns + q : n.turns + q + 1, :]
@@ -267,9 +268,9 @@
         else:
             cosines[n.turns - q] = cosines[n.turns - q] + a
             sines[n.turns - q] = sines[n.turns - q] - b
-    start = pl.multiple_of(band * (TILE * n.rows), TILE * n.rows)
+    start = pl.multiple_of(band * (size * n.rows), size * n.rows)
     for s, part in enumerate(cell_sums(n, cosines, sines)):
-        field[pl.ds(start + s, TILE, stride=n.rows), :] = part
+        field[pl.ds(start + s, size, stride=n.rows), :] = part
 
 
 def kernel(n, listed, placed, orbital, external, *refs):
@@ -443,22 +444,26 @@
         dens_copy(peer, team).start()
 
     low = (me < owners // 2).astype(jnp.int32)
-    far_bands = [low * (n.bands - 1 - k) + (1 - low) * k for k in range(n.bands)]
+
+    def far_bands(size):
+        count = n.levels // size
+        return [low * (count - 1 - k) + (1 - low) * k for k in range(count)]
+
     rho_base = 2
     field_base = rho_base + 2 * n.each
     grad_base = field_base + 2 * n.each
     field_in = []
     for turn in range(n.each):
-        for band in reversed(far_bands):
-            for index in range(n.share):
-                peer = band * n.share + index
+        for band in reversed(far_bands(n.ahead)):
+            for index in range(n.ahead // depth):
+                peer = band * (n.ahead // depth) + index
                 rho[rows_of(peer), :] = take_coded(rho_base + 2 * turn, peer, peer * n.each + turn, rho_land, rho_steps)
-            forward_band(n, rho, band, planes, lane, twiddle)
+            forward_band(n, rho, band, n.ahead, planes, lane, twiddle)
         along_z(planes, to_waves, from_waves, green)
-        for band in far_bands:
-            back_band(n, planes, band, field_flat, lane_back, twiddle)
-            for index in range(n.share):
-                peer = band * n.share + index
+        for band in far_bands(n.behind):
+            back_band(n, planes, band, n.behind, field_flat, lane_back, twiddle)
+            for index in range(n.behind // depth):
+                peer = band * (n.behind // depth) + index
                 slot = peer * n.each + turn
                 here, there = (slot, field_send, field_step), (me * n.each + turn, field_land, field_steps)
                 field_in += send_coded(field_base + 2 * turn, peer, field_flat[rows_of(peer), :], here, there)

time: 25.2 us -> 24.8 us (0.984)
  Pallas kernels: 24.3 us -> 24 us
    pallas_call x1, Pallas kernels: 24.3 us -> 24 us  [body(): pl.pallas_call(functools.partial(kernel, n), out_shape=VMEM((flat_rows, L...]
where the time goes in v6:
time: 24.8 us; the launch traced here: 24.7 us
  Pallas kernels  24 us (97%)
  local copies, waits for them, and re-layouts  0.68 us (3%)
    pallas_call x1, Pallas kernels, body(): pl.pallas_call(functools.partial(kernel, n), out_shape=VMEM((flat_rows, L...  24 us
    reshape x1, local copies, waits for them, and re-layouts, body(): return slab_out.reshape(1, levels, cells)  0.68 us

profile of v6, /device:TPU:0, one launch (start us, length us, event | category | flops | bytes accessed | tf_op | source)
XLA Modules:
  0.0 24.7 jit_solution(2971663523393014424)
XLA Ops:
  0.0 24.0 %gradient.1 = f32[256,128]{1,0:T(8,128)S(1)} custom-call(s32[2,8]{1,0:T(2,128)} %bitcast.3, s32[1,2]{1,0:T(1,128)} %placed.1, bf16[32,1024]{1,0:T(8,128)(2,1)} %bitcast.2, bf16[32,4096]{1,0:T(8,128)(2,1)} %external.1, bf16[64,96]{1,0:T(8,128)(2,1)} %constant.16.clone.refs_0_, bf16[32,192]{1,0:T(8,128)(2,1)} %constant.17.clone.refs_1_, ...), custom_call_target="tpu_custom_call" | custom-call | tf_op jit(solution)/shard_map/gradient/pallas_call | solution.py:565
  24.0 0.7 %reshape.3 = f32[1,32,1024]{2,1,0:T(8,128)} reshape(f32[256,128]{1,0:T(8,128)S(1)} %gradient.1) | data formatting | bytes 262144 | tf_op jit(solution)/shard_map/reshape | solution.py:574

commit v7 on v6

--- a/solution.py
+++ b/solution.py
@@ -109,7 +109,7 @@
 def encode(value):
     largest = jnp.max(jnp.abs(value), axis=0, keepdims=True)
     largest = jnp.maximum(largest, TINY)
-    code = jnp.round(value * (STEPS / largest)).astype(jnp.int32)
+    code = (value * (STEPS / largest) + (STEPS + 1.5)).astype(jnp.int32) - (int(STEPS) + 1)
     return code.astype(CODE), largest * (1.0 / STEPS)
 
 
@@ -385,13 +385,13 @@
         boxes_in[-1].start()
     sent += boxes_in
     arrived(0, place_send, lambda peer: place_land.at[peer])
-    arrived(1, box_send.at[0], lambda peer: box_land.at[peer])
     for owner in range(owners):
         corner[owner, 0] = place_land[owner, 0, 0]
         corner[owner, 1] = place_land[owner, 0, 1]
         for turn in range(n.each):
             pairs[owner * n.each + turn, 0] = place_land[owner, 0, 2 + 2 * turn]
             pairs[owner * n.each + turn, 1] = place_land[owner, 0, 3 + 2 * turn]
+    arrived(1, box_send.at[0], lambda peer: box_land.at[peer])
 
     def shift_of(row):
         first, second = pairs[row, 0], pairs[row, 1]

time: 24.8 us -> 24.7 us (level)
  no operation moved by 1% of the time
where the time goes in v7:
time: 24.7 us; the launch traced here: 24.6 us
  Pallas kernels  23.9 us (97%)
  local copies, waits for them, and re-layouts  0.68 us (3%)
    pallas_call x1, Pallas kernels, body(): pl.pallas_call(functools.partial(kernel, n), out_shape=VMEM((flat_rows, L...  23.9 us
    reshape x1, local copies, waits for them, and re-layouts, body(): return slab_out.reshape(1, levels, cells)  0.68 us

profile of v7, /device:TPU:0, one launch (start us, length us, event | category | flops | bytes accessed | tf_op | source)
XLA Modules:
  0.0 24.6 jit_solution(13867821794039675128)
XLA Ops:
  0.0 23.9 %gradient.1 = f32[256,128]{1,0:T(8,128)S(1)} custom-call(s32[2,8]{1,0:T(2,128)} %bitcast.3, s32[1,2]{1,0:T(1,128)} %placed.1, bf16[32,1024]{1,0:T(8,128)(2,1)} %bitcast.2, bf16[32,4096]{1,0:T(8,128)(2,1)} %external.1, bf16[64,96]{1,0:T(8,128)(2,1)} %constant.16.clone.refs_0_, bf16[32,192]{1,0:T(8,128)(2,1)} %constant.17.clone.refs_1_, ...), custom_call_target="tpu_custom_call" | custom-call | tf_op jit(solution)/shard_map/gradient/pallas_call | solution.py:565
  23.9 0.7 %reshape.3 = f32[1,32,1024]{2,1,0:T(8,128)} reshape(f32[256,128]{1,0:T(8,128)S(1)} %gradient.1) | data formatting | bytes 262144 | tf_op jit(solution)/shard_map/reshape | solution.py:574

commit v8 on v7

--- a/solution.py
+++ b/solution.py
@@ -134,6 +134,13 @@
     above = pltpu.roll(turned, lax.rem(down + 1, rows), axis=1)
     lane = lax.broadcasted_iota(jnp.int32, value.shape, 2)
     return jnp.where(lane >= carried, here, above)
+
+
+def carry(n, value, shift_y, shift_x):
+    shape = value.shape
+    value = value.reshape(shape[0] // n.rows, n.rows, LANES)
+    amount = lax.rem(shift_y * n.side + shift_x + 2 * n.cells, n.cells)
+    return flat_roll(value, amount).reshape(shape)
 
 
 def slide(n, value, shift_y, shift_x):
@@ -404,10 +411,12 @@
             dy, dx = shift_of(row)
             a = box_land[pairs[row, 0]].astype(F32)
             b = slide(n, box_land[pairs[row, 1]].astype(F32), dy, dx)
-            near[row] = a
             moved[row] = b
             rho_in += send_coded(2 + 2 * turn, peer, a * b, (row, rho_send, rho_step), (me * n.each + turn, rho_land, rho_steps))
     sent += rho_in
+    for row in range(n.pairs):
+        dy, dx = shift_of(row)
+        near[row] = slide(n, box_land[pairs[row, 0]].astype(F32), -dy, -dx)
 
     for item in table_in:
         item.wait()
@@ -505,7 +514,7 @@
             dy, dx = shift_of(row)
             field = take_coded(field_base + 2 * turn, peer, row, field_land, field_steps) * MIXING
             moved[row] = field * moved[row]
-            near[row] = slide(n, field * near[row], -dy, -dx)
+            near[row] = carry(n, field, -dy, -dx) * near[row]
     for peer in peers:
         total = read[peer]
         for row in range(n.pairs):

time: 24.7 us -> 24.7 us (level)
  no operation moved by 1% of the time
where the time goes in v8:
time: 24.7 us; the launch traced here: 24.6 us
  Pallas kernels  23.9 us (97%)
  local copies, waits for them, and re-layouts  0.68 us (3%)
    pallas_call x1, Pallas kernels, body(): pl.pallas_call(functools.partial(kernel, n), out_shape=VMEM((flat_rows, L...  23.9 us
    reshape x1, local copies, waits for them, and re-layouts, body(): return slab_out.reshape(1, levels, cells)  0.68 us

profile of v8, /device:TPU:0, one launch (start us, length us, event | category | flops | bytes accessed | tf_op | source)
XLA Modules:
  0.0 24.6 jit_solution(8210864148535291360)
XLA Ops:
  0.0 23.9 %gradient.1 = f32[256,128]{1,0:T(8,128)S(1)} custom-call(s32[2,8]{1,0:T(2,128)} %bitcast.3, s32[1,2]{1,0:T(1,128)} %placed.1, bf16[32,1024]{1,0:T(8,128)(2,1)} %bitcast.2, bf16[32,4096]{1,0:T(8,128)(2,1)} %external.1, bf16[64,96]{1,0:T(8,128)(2,1)} %constant.16.clone.refs_0_, bf16[32,192]{1,0:T(8,128)(2,1)} %constant.17.clone.refs_1_, ...), custom_call_target="tpu_custom_call" | custom-call | tf_op jit(solution)/shard_map/gradient/pallas_call | solution.py:574
  23.9 0.7 %reshape.3 = f32[1,32,1024]{2,1,0:T(8,128)} reshape(f32[256,128]{1,0:T(8,128)S(1)} %gradient.1) | data formatting | bytes 262144 | tf_op jit(solution)/shard_map/reshape | solution.py:583
